TPU v7x, 128 devices: a whole 4x4x4 slice. The times are simulated.
128 devices in a mesh: judge: 4 (over y_hi, core), fsdp: 32 (over y_lo, x, z).
Axes of the slice: x: 4, y: 4 (y_hi: 2, y_lo: 2; y = y_hi * 2 + y_lo), z: 4, core: 2. Of those that a mesh axis runs over, the one named last changes fastest.
Arguments:
- hidden: bfloat16 [4, 32768, 4096], P('judge', 'fsdp'), may hold values from -32 to 32
- lengths: int32 [64], replicated, may hold values from 128 to 512
- duplicate_group_index: int32 [64], replicated, may hold values from 0 to 15, as said below
- attn_gain: bfloat16 [4, 4096], P('judge', 'fsdp'), may hold values from 0.5 to 1.5
- w_query: bfloat16 [4, 4096, 4096], P('judge', None, 'fsdp'), may hold values from -1 to 1
- w_key: bfloat16 [4, 4096, 1024], P('judge', 'fsdp'), may hold values from -1 to 1
- w_value: bfloat16 [4, 4096, 1024], P('judge', 'fsdp'), may hold values from -0.09375 to 0.09375
- w_out: bfloat16 [4, 4096, 4096], P('judge', 'fsdp'), may hold values from -0.09375 to 0.09375
- mlp_gain: bfloat16 [4, 4096], P('judge', 'fsdp'), may hold values from 0.5 to 1.5
- w_gate: bfloat16 [4, 4096, 14336], P('judge', None, 'fsdp'), may hold values from -0.09375 to 0.09375
- w_up: bfloat16 [4, 4096, 14336], P('judge', None, 'fsdp'), may hold values from -0.09375 to 0.09375
- w_down: bfloat16 [4, 14336, 4096], P('judge', 'fsdp'), may hold values from -0.046875 to 0.046875
- final_gain: bfloat16 [4, 4096], P('judge', 'fsdp'), may hold values from 0.5 to 1.5
- reward_head: float32 [4, 4096], P('judge'), may hold values from -8 to 8
Outputs:
- survivor_weights: float32 [64], replicated
- cluster_features: float32 [16, 4096], P(None, 'fsdp')
Inputs may be any that keep to these rules, and one draw needn't show every extreme that they name: `duplicate_group_index`: every cluster holds exactly four candidates.
All inputs are finite; a program needn't handle non-finite values.
Results may differ from a plain program's by a relative error of at most 0.003.
Values may be sent and summed in bfloat16 or wider, within the bound.
No kernel may reach another device: no remote copies, remote signals or barrier semaphores. Data moves between devices by JAX's collectives and lax.ppermute only.
A program may use at most 192 MiB of HBM per device.

v0:
```python
import math

import jax
import jax.numpy as jnp
from jax import lax
from jax.sharding import PartitionSpec as P

KV_HEADS = 8
HEAD_DIM = 128
LEN = 512


EPS = 1e-05
ROPE_BASE = 500000.0


def in_order(blocks, dim):
    dims = list(blocks.shape[1:])
    dims[dim] *= blocks.shape[0]
    return jnp.moveaxis(blocks, 0, dim).reshape(dims)


def gather_packed(arrays, axis, dims):
    ravelled = jnp.concatenate([a.reshape(-1) for a in arrays])
    lines, at, done = (lax.all_gather(ravelled, axis), 0, [])
    for a, dim in zip(arrays, dims):
        blocks = lines[:, at : at + a.size].reshape(-1, *a.shape)
        done.append(in_order(blocks, dim))
        at += a.size
    return tuple(done)


def sent_together(arrays, axis, dim, along):
    both = jnp.concatenate(arrays, axis=along)
    filled, at, done = (lax.all_gather(both, axis, axis=dim, tiled=True), 0, [])
    for a in arrays:
        done.append(lax.slice_in_dim(filled, at, at + a.shape[along], axis=along))
        at += a.shape[along]
    return tuple(done)


def cut_along(x, dim, peers):
    before, after = (x.shape[:dim], x.shape[dim + 1 :])
    return jnp.moveaxis(x.reshape(*before, peers, -1, *after), dim, 0)


def sum_at_owner(x, axis, dim):
    peers = lax.axis_size(axis)
    blocks = lax.all_to_all(cut_along(x, dim, peers), axis, 0, 0, tiled=True)
    return jnp.sum(blocks, axis=0)


def rows_for(lines, peers):
    spare = -lines.shape[0] % peers
    if not spare:
        return lines
    return jnp.concatenate([lines, jnp.zeros((spare, *lines.shape[1:]), lines.dtype)])


def from_everyone(x, axis):
    peers = lax.axis_size(axis)
    return lax.all_to_all(jnp.broadcast_to(x[None], (peers, *x.shape)), axis, 0, 0, tiled=True)


def gather_directly(x, axis, dim):
    blocks = from_everyone(x, axis)
    return in_order(blocks, dim)


def total_of(x, axes):
    lines = x.reshape(-1, x.shape[-1])
    own = sum_at_owner(rows_for(lines, lax.axis_size(axes)), axes, 0)
    whole = gather_directly(own, axes, 0)
    return whole[: len(lines)].reshape(x.shape)


def taken_together(x, axis):
    return from_everyone(x, axis).sum(axis=0)


def packed_total(arrays, axis):
    ends = [0]
    for a in arrays:
        ends.append(ends[-1] + a.size)
    running = taken_together(jnp.concatenate([a.ravel() for a in arrays]), axis)
    return tuple((running[b:e].reshape(a.shape) for a, b, e in zip(arrays, ends, ends[1:])))


def row_scale(v):
    return lax.rsqrt(jnp.mean(v * v, axis=-1, keepdims=True) + EPS)


def angles(position):
    half = HEAD_DIM // 2
    freq = jnp.exp(jnp.arange(half, dtype=jnp.float32) * (-2.0 * math.log(ROPE_BASE) / HEAD_DIM))
    turned = position[..., None] * freq
    return (jnp.cos(turned), jnp.sin(turned))


def rotate(v, cosine, sine):
    half = HEAD_DIM // 2
    first = v[..., :half]
    second = v[..., half:]
    return jnp.concatenate(
        [first * cosine - second * sine, second * cosine + first * sine], axis=-1
    )


def remaining_candidates(judge_panel, duplicate_group_index, duplicate_groups):
    same = duplicate_group_index[:, None] == duplicate_group_index[None, :]
    top = jnp.max(jnp.where(same, judge_panel[None, :], -1e30), axis=1)
    expo = jnp.exp(judge_panel - top)
    total = jnp.sum(jnp.where(same, expo[None, :], 0.0), axis=1)
    weight_values = expo / total
    panel_member = (
        duplicate_group_index[:, None] == jnp.arange(duplicate_groups, dtype=jnp.int32)[None, :]
    ).astype(jnp.float32)
    return (weight_values, panel_member)


def body(
    hidden,
    lengths,
    duplicate_group_index,
    attn_gain,
    w_query,
    w_key,
    w_value,
    w_out,
    mlp_gain,
    w_gate,
    w_up,
    w_down,
    final_gain,
    reward_head,
):
    reward_judges = lax.axis_size("judge")
    devices = lax.axis_size("fsdp")
    me = lax.axis_index("fsdp")
    tokens = hidden[0]
    tok_dev, width = tokens.shape
    seq_dev = tok_dev // LEN
    cands = lengths.shape[0]
    duplicate_groups = cands // 4
    groups = width // HEAD_DIM // KV_HEADS
    column_count = width // devices
    col_start = me * column_count
    own_len = lax.dynamic_slice_in_dim(lengths, me * seq_dev, seq_dev)
    last_index = jnp.arange(seq_dev, dtype=jnp.int32) * LEN + own_len - 1
    own_last = tokens[last_index]
    x_last, gain_attn, gain_mlp = gather_packed(
        (own_last, attn_gain[0], mlp_gain[0]), "fsdp", (0, 0, 0)
    )
    gain_final = final_gain[0]
    x_last = x_last.astype(jnp.float32)
    scale = row_scale(tokens.astype(jnp.float32))
    key_rows, value_rows = sent_together((w_key[0], w_value[0]), "fsdp", 0, 1)
    tok_norm = (tokens.astype(jnp.float32) * scale * gain_attn.astype(jnp.float32)).astype(
        jnp.bfloat16
    )
    keys = jnp.dot(tok_norm, key_rows, preferred_element_type=jnp.float32)
    values = jnp.dot(tok_norm, value_rows, preferred_element_type=jnp.float32)
    key_cos, key_sin = angles(jnp.arange(LEN, dtype=jnp.float32))
    keys = keys.reshape(seq_dev, LEN, KV_HEADS, HEAD_DIM)
    keys = rotate(keys, key_cos[None, :, None, :], key_sin[None, :, None, :]).astype(jnp.bfloat16)
    values = values.astype(jnp.bfloat16).reshape(seq_dev, LEN, KV_HEADS, HEAD_DIM)
    q_norm = (x_last * row_scale(x_last) * gain_attn.astype(jnp.float32)).astype(jnp.bfloat16)
    q_part = jnp.dot(q_norm, w_query[0], preferred_element_type=jnp.float32)
    q_part = q_part.reshape(cands, q_part.shape[1] // HEAD_DIM, HEAD_DIM)
    cosine, sine = angles((lengths - 1).astype(jnp.float32))
    q_part = (
        rotate(q_part, cosine[:, None, :], sine[:, None, :]).astype(jnp.bfloat16).reshape(cands, -1)
    )
    q_own = lax.all_to_all(q_part, "fsdp", split_axis=0, concat_axis=1, tiled=True)
    q_own = q_own.reshape(seq_dev, KV_HEADS, groups, HEAD_DIM)
    scores = jnp.einsum(
        "skgd,slkd->skgl", q_own, keys, preferred_element_type=jnp.float32
    ) * HEAD_DIM ** (-0.5)
    valid = jnp.arange(LEN, dtype=jnp.int32)[None, None, None, :] < own_len[:, None, None, None]
    scores = jnp.where(valid, scores, -1e30)
    top = jnp.max(scores, axis=-1, keepdims=True)
    expo = jnp.exp(scores - top)
    probs = (expo / jnp.sum(expo, axis=-1, keepdims=True)).astype(jnp.bfloat16)
    mixed = jnp.einsum("skgl,slkd->skgd", probs, values, preferred_element_type=jnp.float32)
    mixed = mixed.reshape(seq_dev, width).astype(jnp.bfloat16)
    head_rows = lax.all_to_all(mixed, "fsdp", split_axis=1, concat_axis=0, tiled=True)
    attn = total_of(jnp.dot(head_rows, w_out[0], preferred_element_type=jnp.float32), "fsdp")
    after_attn = x_last + attn
    m_norm = (after_attn * row_scale(after_attn) * gain_mlp.astype(jnp.float32)).astype(
        jnp.bfloat16
    )
    gate = jnp.dot(m_norm, w_gate[0], preferred_element_type=jnp.float32)
    up = jnp.dot(m_norm, w_up[0], preferred_element_type=jnp.float32)
    act = (jax.nn.silu(gate) * up).astype(jnp.bfloat16)
    down_terms = jnp.dot(act, w_down[0], preferred_element_type=jnp.float32)
    down_cols = sum_at_owner(down_terms, "fsdp", 1)
    after_cols = lax.dynamic_slice_in_dim(after_attn, col_start, column_count, 1) + down_cols
    head_cols = lax.dynamic_slice_in_dim(reward_head[0], col_start, column_count, 0)
    weighted = after_cols * gain_final.astype(jnp.float32)
    squares, product = packed_total(
        (
            jnp.sum(after_cols * after_cols, axis=1),
            jnp.dot(weighted, head_cols, precision=lax.Precision.HIGHEST),
        ),
        "fsdp",
    )
    col_scale = lax.rsqrt(squares / width + EPS)
    feature_cols = weighted * col_scale[:, None]
    score = product * col_scale
    total_cols, score_total = packed_total((feature_cols, score), "judge")
    weight_values, panel_member = remaining_candidates(
        score_total / reward_judges, duplicate_group_index, duplicate_groups
    )
    cluster_cols = jnp.dot(
        panel_member.T,
        weight_values[:, None] * (total_cols / reward_judges),
        precision=lax.Precision.HIGHEST,
    )
    return (weight_values, cluster_cols)


def solution(mesh):
    in_specs = (
        P("judge", "fsdp", None),
        P(),
        P(),
        P("judge", "fsdp"),
        P("judge", None, "fsdp"),
        P("judge", "fsdp", None),
        P("judge", "fsdp", None),
        P("judge", "fsdp", None),
        P("judge", "fsdp"),
        P("judge", None, "fsdp"),
        P("judge", None, "fsdp"),
        P("judge", "fsdp", None),
        P("judge", "fsdp"),
        P("judge", None),
    )
    out_specs = (P(), P(None, "fsdp"))
    return jax.shard_map(body, mesh=mesh, in_specs=in_specs, out_specs=out_specs, check_vma=False)
```

profile of v0, /device:TPU:1, one launch (start us, length us, event | category | flops | bytes accessed | tf_op | source)
XLA Modules:
  0.0 385.3 jit_solution(3134053307039716645)
XLA Ops:
  7.2 0.0 all-gather.4.cloned.1.call-start
  7.2 2.0 pad_maximum_fusion
  9.2 0.0 all-gather.4.cloned.1.call-update
  9.2 0.7 compare_select_fusion.2
  10.0 5.0 %gather_fusion = bf16[2,4096]{1,0:T(2,128)(2,1)S(1)} fusion(bf16[1024,4096]{1,0:T(8,128)(2,1)} %bitcast.116, s32[1024]{0:T(1024)S(1)} %pad_clamp_fusion), kind=kCustom, calls=%fused_computation | custom fusion | bytes 32776 | tf_op jit(solution)/shard_map/gather | solution.py:150
  15.1 0.7 pad_maximum_fusion.2
  15.8 93.5 %all-gather.1 = bf16[32,1,8448]{2,1,0:T(2,128)(2,1)S(1)} all-gather(bf16[1,1,8448]{2,1,0:T(2,128)(2,1)S(1)} %reshape.357), channel_id=2, replica_groups=mesh['judge'=4,'fsdp'=32] {'fsdp'}, dimensions={0}, use_global_device_ids=true | all-gather | bytes 557568 | tf_op jit(solution)/shard_map/all_gather | solution.py:25
  109.2 0.1 copy.78
  109.4 0.1 slice_convert_fusion
  109.4 1.1 reshape.342
  110.6 1.4 multiply_reduce_fusion.1
  112.0 0.1 rsqrt.33
  112.1 0.3 mul.274
  112.5 0.6 copy.60
  113.1 0.1 multiply_convert_fusion.2
  113.2 0.2 convert_element_type.110
  113.4 1.6 convolution_bitcast_fusion
  115.0 0.2 fusion.70
  115.2 0.7 pad_maximum_fusion.3
  115.9 4.0 %all-to-all-start = ((bf16[32,2,128]{2,1,0:T(2,128)(2,1)}), bf16[32,2,128]{2,1,0:T(2,128)(2,1)S(1)}, u32[]{:S(2)}, u32[]{:S(2)}) async-start(bf16[32,2,128]{2,1,0:T(2,128)(2,1)} %pad_maximum_fusion.3), calls=%async_computation | async-start | bytes 32768 | tf_op jit(solution)/shard_map/all_to_all | solution.py:174
  119.9 5.2 %fusion.1 = f32[1024]{0:T(1024)S(1)} fusion(bf16[1,1024,4096]{2,1,0:T(8,128)(2,1)} %param.14), kind=kLoop, calls=%fused_computation.4 | loop fusion | flops 12581888 | bytes 8392704 | tf_op jit(solution)/shard_map/reduce_sum | solution.py:90
  125.1 0.5 fusion.60
  125.6 10.4 %multiply_convert_fusion = bf16[1,1024,4096]{2,1,0:T(8,128)(2,1)} fusion(bf16[1,1024,4096]{2,1,0:T(8,128)(2,1)} %param.14, f32[4096]{0:T(1024)S(1)} %get-tuple-element.13, f32[1024]{0:T(1024)S(1)} %add_rsqrt_fusion.1), kind=kLoop, calls=%fused_computation.7 | loop fusion | flops 16777216 | bytes 16797696 | tf_op jit(solution)/shard_map/convert_element_type | solution.py:158
  136.0 0.1 iota_compare_fusion.2
  136.1 77.0 %all-gather.4.cloned.1.call-done = bf16[4096,2048]{1,0:T(8,128)(2,1)} async-done(((bf16[128,2048]{1,0:T(8,128)(2,1)}), bf16[4096,2048]{1,0:T(8,128)(2,1)}) %all-gather.4.cloned.1.call-update) | async-done | bytes 16777232 | tf_op jit(solution)/shard_map/all_gather | solution.py:35
  213.1 7.6 %slice_bitcast_fusion = bf16[1024,4096]{0,1:T(8,128)(2,1)} fusion(bf16[4096,2048]{1,0:T(8,128)(2,1)} %all-gather.4.cloned.1.call-done), kind=kLoop, calls=%fused_computation.10 | loop fusion | bytes 16777216 | tf_op jit(solution)/shard_map/dot_general | solution.py:161
  220.7 12.0 %copy.43 = bf16[1024,4096]{1,0:T(8,128)(2,1)} copy(bf16[1024,4096]{0,1:T(8,128)(2,1)} %slice_bitcast_fusion) | data formatting | bytes 16777216 | tf_op jit(solution)/shard_map/dot_general | solution.py:161
  232.7 13.9 %convert_bitcast_fusion = bf16[128,8,8,128]{3,1,2,0:T(8,128)(2,1)S(1)} fusion(bf16[4096,2048]{1,0:T(8,128)(2,1)} %all-gather.4.cloned.1.call-done, f32[4096]{0:T(1024)S(1)} %get-tuple-element.13, f32[1024]{0:T(1024)S(1)} %add_rsqrt_fusion.1, bf16[1,1024,4096]{2,1,0:T(8,128)(2,1)} %param.14), kind=kOutput, calls=%fused_computation.26 | convolution fusion | flops 8607760384 | bytes 18894848 | tf_op jit(solution)/shard_map/dot_general | solution.py:162
  246.6 2.0 copy.62
  248.6 11.4 %fusion.103 = f32[2,512,8,128]{1,3,2,0:T(8,128)S(1)} fusion(bf16[2,512,4096,1]{2,1,3,0:T(8,128)(2,1)} %bitcast.117, bf16[8,128,4096,1]{2,1,0,3:T(8,128)(2,1)S(1)} %bitcast.118), kind=kOutput, calls=%fused_computation.122 | convolution fusion | flops 8589934592 | bytes 20971520 | tf_op jit(solution)/shard_map/dot_general | solution.py:161
  260.0 1.7 subtract_convert_fusion
  261.8 1.8 fusion.100
  263.5 2.1 fusion.46
  265.7 11.7 %all_to_all.53 = bf16[2,32,128]{2,0,1:T(2,128)(2,1)S(1)} all-to-all(bf16[2,32,128]{2,0,1:T(2,128)(2,1)S(1)} %copy.46), channel_id=1, replica_groups=mesh['judge'=4,'fsdp'=32] {'fsdp'}, dimensions={1} | all-to-all | bytes 32768 | tf_op jit(solution)/shard_map/all_to_all | solution.py:186
  277.4 0.3 fusion.49
  277.7 0.8 copy.48
  278.5 15.5 %all_to_all.54 = f32[32,2,4096]{2,1,0:T(2,128)S(1)} all-to-all(f32[32,2,4096]{2,1,0:T(2,128)S(1)} %copy.48), channel_id=1, replica_groups=mesh['judge'=4,'fsdp'=32] {'fsdp'}, dimensions={0} | all-to-all | bytes 2097152 | tf_op jit(solution)/shard_map/all_to_all | solution.py:49
  294.0 0.3 reduce_sum.93
  294.4 1.5 broadcast_in_dim.39
  295.9 7.1 %all-to-all-start.3 = ((f32[32,2,4096]{2,1,0:T(2,128)}), f32[32,2,4096]{2,1,0:T(2,128)S(1)}, u32[]{:S(2)}, u32[]{:S(2)}) async-start(f32[32,2,4096]{2,1,0:T(2,128)} %broadcast_in_dim.39), calls=%async_computation.3 | async-start | bytes 2097152 | tf_op jit(solution)/shard_map/all_to_all | solution.py:62
  303.0 1.9 reshape.344
  304.9 11.8 %all-to-all-done.3 = f32[32,2,4096]{2,1,0:T(2,128)S(1)} async-done(((f32[32,2,4096]{2,1,0:T(2,128)}), f32[32,2,4096]{2,1,0:T(2,128)S(1)}, u32[]{:S(2)}, u32[]{:S(2)}) %all-to-all-start.3) | async-done | bytes 1048608 | tf_op jit(solution)/shard_map/all_to_all | solution.py:62
  316.7 2.0 multiply_reduce_fusion
  318.6 0.6 multiply_convert_fusion.1
  319.3 0.2 convert_element_type.126
  319.5 3.2 fusion.14
  322.7 6.3 %fusion.26 = f32[32,64,128]{2,1,0:T(8,128)} fusion(bf16[64,4096]{1,0:T(8,128)(2,1)S(1)} %convert_element_type.126, bf16[1,4096,448]{1,2,0:T(8,128)(2,1)} %param.24, f32[64,448]{1,0:T(8,128)S(1)} %fusion.14, bf16[1,448,4096]{2,1,0:T(8,128)(2,1)} %param.25), kind=kOutput, calls=%fused_computation.29 | convolution fusion | flops 469934080 | bytes 9027584 | tf_op jit(solution)/shard_map/dot_general | solution.py:195
  329.0 6.7 %all-to-all-start.4 = ((f32[32,64,128]{2,1,0:T(8,128)}), f32[32,64,128]{2,1,0:T(8,128)S(1)}, u32[]{:S(2)}, u32[]{:S(2)}) async-start(f32[32,64,128]{2,1,0:T(8,128)} %fusion.26), calls=%async_computation.4 | async-start | bytes 2097152 | tf_op jit(solution)/shard_map/all_to_all | solution.py:49
  335.8 1.7 reshape.339
  337.5 13.1 %all-to-all-done.4 = f32[32,64,128]{2,1,0:T(8,128)S(1)} async-done(((f32[32,64,128]{2,1,0:T(8,128)}), f32[32,64,128]{2,1,0:T(8,128)S(1)}, u32[]{:S(2)}, u32[]{:S(2)}) %all-to-all-start.4) | async-done | bytes 1048608 | tf_op jit(solution)/shard_map/all_to_all | solution.py:49
  350.6 0.1 reduce_sum.95
  350.7 0.9 multiply_reduce_fusion.2
  351.6 0.8 convolution_bitcast_fusion.1
  352.4 0.1 pad_maximum_fusion.4
  352.5 12.5 %all_to_all.55 = f32[32,1,128]{2,1,0:T(1,128)S(1)} all-to-all(f32[32,1,128]{2,1,0:T(1,128)S(1)} %broadcast_in_dim.40), channel_id=1, replica_groups=mesh['judge'=4,'fsdp'=32] {'fsdp'}, dimensions={0} | all-to-all | bytes 32768 | tf_op jit(solution)/shard_map/all_to_all | solution.py:62
  365.0 0.1 add_rsqrt_fusion.2
  365.1 0.1 multiply_bitcast_fusion
  365.2 0.1 broadcast_in_dim.41
  365.3 11.2 %all_to_all.56 = f32[4,1,8256]{2,1,0:T(1,128)S(1)} all-to-all(f32[4,1,8256]{2,1,0:T(1,128)S(1)} %broadcast_in_dim.41), channel_id=1, replica_groups=mesh['judge'=4,'fsdp'=32] {'judge'}, dimensions={0} | all-to-all | bytes 264192 | tf_op jit(solution)/shard_map/all_to_all | solution.py:62
  376.5 0.1 reduce_sum.98
  376.7 0.2 fusion.67
  376.9 0.2 fusion.68
  377.1 0.5 broadcast_multiply_fusion
  377.6 0.9 fusion.74
  (30 shorter events, 0.2 us)
Async XLA Ops:
  7.2 270.2 %copy-start = (bf16[1,128,4096]{2,1,0:T(8,128)(2,1)S(1)}, bf16[1,128,4096]{2,1,0:T(8,128)(2,1)}, u32[]{:S(2)}) copy-start(bf16[1,128,4096]{2,1,0:T(8,128)(2,1)} %param.21) | copy-start | bytes 3145732
  7.2 206.0 %all-gather.4.cloned.1.call-start = ((), (), s32[]{:S(2)}) async-start(), calls=%async_computation.7 | async-start | bytes 17301504 | tf_op jit(solution)/shard_map/all_gather | solution.py:35
  112.0 3.0 copy-start.3
  115.9 20.2 %all-to-all-start = ((bf16[32,2,128]{2,1,0:T(2,128)(2,1)}), bf16[32,2,128]{2,1,0:T(2,128)(2,1)S(1)}, u32[]{:S(2)}, u32[]{:S(2)}) async-start(bf16[32,2,128]{2,1,0:T(2,128)(2,1)} %pad_maximum_fusion.3), calls=%async_computation | async-start | bytes 32768 | tf_op jit(solution)/shard_map/all_to_all | solution.py:174
  232.7 15.9 %copy-start.1 = (bf16[1024,4096]{1,0:T(8,128)(2,1)S(1)}, bf16[1024,4096]{1,0:T(8,128)(2,1)}, u32[]{:S(2)}) copy-start(bf16[1024,4096]{1,0:T(8,128)(2,1)} %copy.43) | copy-start | bytes 25165828
  295.9 20.8 %all-to-all-start.3 = ((f32[32,2,4096]{2,1,0:T(2,128)}), f32[32,2,4096]{2,1,0:T(2,128)S(1)}, u32[]{:S(2)}, u32[]{:S(2)}) async-start(f32[32,2,4096]{2,1,0:T(2,128)} %broadcast_in_dim.39), calls=%async_computation.3 | async-start | bytes 2097152 | tf_op jit(solution)/shard_map/all_to_all | solution.py:62
  322.7 13.1 %copy-start.4 = (bf16[1,128]{1,0:T(2,128)(2,1)S(1)}, bf16[1,128]{1,0:T(2,128)(2,1)}, u32[]{:S(2)}) copy-start(bf16[1,128]{1,0:T(2,128)(2,1)} %param.26) | copy-start | bytes 772
  329.0 47.6 %copy-start.2 = (s32[64]{0:T(128)S(1)}, s32[64]{0:T(128)}, u32[]{:S(2)}) copy-start(s32[64]{0:T(128)} %param.16) | copy-start | bytes 772
  329.0 21.6 %all-to-all-start.4 = ((f32[32,64,128]{2,1,0:T(8,128)}), f32[32,64,128]{2,1,0:T(8,128)S(1)}, u32[]{:S(2)}, u32[]{:S(2)}) async-start(f32[32,64,128]{2,1,0:T(8,128)} %fusion.26), calls=%async_computation.4 | async-start | bytes 2097152 | tf_op jit(solution)/shard_map/all_to_all | solution.py:49
Sparse Core Ops, SparseCore 0:
  9.6 203.4 all-gather.3
where the time goes:
time: 387 us; the launch traced here: 385 us
  blocking collectives  145 us (37%)
  waiting for transfers between devices  102 us (26%)
  matrix products  42.3 us (11%)
  local copies, waits for them, and re-layouts  35.3 us (9%)
  other arithmetic  29.1 us (8%)
  starting transfers between devices  17.9 us (5%)
  between operations  14.4 us (4%)
    all_gather x1, blocking collectives, gather_packed(): lines, at, done = (lax.all_gather(ravelled, axis), 0, [])  93.5 us
    all_gather x1, waiting for transfers between devices, sent_together(): filled, at, done = (lax.all_gather(both, axis, axis=dim, tiled=True), 0, [])  77 us
    all_to_all x2, blocking collectives, from_everyone(): lax.all_to_all(jnp.broadcast_to(x[None], (peers, *x.shape)), axis, 0, 0,...  23.8 us
    dot_general x2, local copies, waits for them, and re-layouts, body(): keys = jnp.dot(tok_norm, key_rows, preferred_element_type=jnp.float32)  19.5 us
    all_to_all x1, blocking collectives, sum_at_owner(): blocks = lax.all_to_all(cut_along(x, dim, peers), axis, 0, 0, tiled=True)  15.5 us
    dot_general x1, matrix products, body(): values = jnp.dot(tok_norm, value_rows, preferred_element_type=jnp.float32)  13.9 us
    all_to_all x1, waiting for transfers between devices, sum_at_owner(): blocks = lax.all_to_all(cut_along(x, dim, peers), axis, 0, 0, tiled=True)  13.1 us
    all_to_all x1, waiting for transfers between devices, from_everyone(): lax.all_to_all(jnp.broadcast_to(x[None], (peers, *x.shape)), axis, 0, 0,...  11.8 us
  transfers between devices with their start and end apart: 4, of which 3 were waited for; matrix products, arithmetic and copies ran while one was open for 9% of the time, Pallas kernels for 0%

commit v1 on v0

v1 whole, which is shorter than its diff:
```python
import math

import jax
import jax.numpy as jnp
from jax import lax
from jax.experimental import pallas as pl
from jax.experimental.pallas import tpu as pltpu
from jax.sharding import PartitionSpec as P


KV_HEADS = 8
HEAD_DIM = 128
LEN = 512
EPS = 1e-05
ROPE_BASE = 500000.0
NY, NX, NZ = 2, 4, 4
GROUP = NY * NX * NZ


OWN_LIMIT = 16 << 20
SMALL_LIMIT = 12 << 20
NEAR_LIMIT = 16 << 20
ATTEND_LIMIT = 20 << 20


def place(y, x, z):
    return ((y % NY) * NX + x % NX) * NZ + z % NZ


def moved(v, dy=0, dx=0, dz=0):
    pairs = [
        (place(y, x, z), place(y + dy, x + dx, z + dz))
        for y in range(NY)
        for x in range(NX)
        for z in range(NZ)
    ]
    return lax.ppermute(v, "fsdp", pairs)


def along(v, name, step):
    return moved(v, **{name: step})


def small_ring(v, name):
    after = along(v, name, -1)
    before = along(v, name, 1)
    opposite = along(v, name, 2)
    return jnp.stack([v, after]), jnp.stack([opposite, before])


def large_ring(low, high, name):
    before_low = along(low, name, 1)
    after_high = along(high, name, -1)
    before_high = along(high, name, 1)
    after_low = along(low, name, -1)
    far = (along(before_low, name, 1), along(after_high, name, -1))
    return (after_low, after_high, before_low, before_high), far


def exchanged(x, axis):
    return lax.all_to_all(x, axis, 0, 0, tiled=True)


def row_scale(v):
    return lax.rsqrt(jnp.mean(v * v, axis=-1, keepdims=True) + EPS)


def angles(position):
    half = HEAD_DIM // 2
    freq = jnp.exp(jnp.arange(half, dtype=jnp.float32) * (-2.0 * math.log(ROPE_BASE) / HEAD_DIM))
    turned = position[..., None] * freq
    return (jnp.cos(turned), jnp.sin(turned))


def rotate(v, cosine, sine):
    half = HEAD_DIM // 2
    first = v[..., :half]
    second = v[..., half:]
    return jnp.concatenate(
        [first * cosine - second * sine, second * cosine + first * sine], axis=-1
    )


def column_of(pos_ref, zo, xo, yo):
    y = lax.rem(pos_ref[0] + yo, NY)
    x = lax.rem(pos_ref[1] + xo, NX)
    z = lax.rem(pos_ref[2] + zo, NZ)
    return pl.multiple_of(((y * NX + x) * NZ + z) * 128, 128)


def pack_kernel(dev_ref, len_ref, x0_ref, x1_ref, ga_ref, gm_ref, gf_ref, out_ref, own_ref):
    width = x0_ref.shape[1]
    peers = out_ref.shape[0]
    rows = []
    for i, x_ref in enumerate((x0_ref, x1_ref)):
        slot = lax.rem(len_ref[2 * dev_ref[0] + i] - 1, 16)
        x = x_ref[...].astype(jnp.float32)
        own = lax.broadcasted_iota(jnp.int32, x.shape, 0) == slot
        rows.append(jnp.sum(jnp.where(own, x, 0.0), axis=0, keepdims=True))
    own_ref[...] = jnp.concatenate(rows, axis=0)
    gains = [g[...].astype(jnp.float32) for g in (ga_ref, gm_ref, gf_ref)]
    first = jnp.concatenate([rows[0], gains[0], gains[2]], axis=1)
    second = jnp.concatenate([rows[1], gains[1], gains[1]], axis=1)
    both = jnp.concatenate([first, second], axis=0).astype(jnp.bfloat16)
    out_ref[...] = jnp.broadcast_to(both[None], (peers, 2, width + 256))


def pack_last(dev, lengths, tokens, attn_gain, mlp_gain, final_gain, peers):
    width = tokens.shape[1]

    def row_block(i):
        return pl.BlockSpec(
            (16, width), lambda s, d, n: ((i * LEN + n[2 * d[0] + i] - 1) // 16, 0)
        )

    gain = pl.BlockSpec((1, 128), lambda s, d, n: (0, 0))
    return pl.pallas_call(
        pack_kernel,
        out_shape=(
            jax.ShapeDtypeStruct((peers, 2, width + 256), jnp.bfloat16),
            jax.ShapeDtypeStruct((2, width), jnp.float32),
        ),
        grid_spec=pltpu.PrefetchScalarGridSpec(
            num_scalar_prefetch=2,
            grid=(1,),
            in_specs=[row_block(0), row_block(1), gain, gain, gain],
            out_specs=(
                pl.BlockSpec((peers, 2, width + 256), lambda s, d, n: (0, 0, 0)),
                pl.BlockSpec((2, width), lambda s, d, n: (0, 0)),
            ),
        ),
        name="pack_last",
    )(dev, lengths, tokens, tokens, attn_gain, mlp_gain, final_gain)


def columns(x_ref, rows, dev_ref, blocks):
    parts = []
    for zo, xo in blocks:
        for yo in range(NY):
            parts.append(x_ref[rows, pl.ds(column_of(dev_ref, zo, xo, yo), 128)])
    return jnp.concatenate(parts, axis=1)


def times(lhs, low, high):
    half = lhs.shape[1] // 2
    return jnp.dot(
        lhs[:, :half], low[...].reshape(half, -1), preferred_element_type=jnp.float32
    ) + jnp.dot(lhs[:, half:], high[...].reshape(half, -1), preferred_element_type=jnp.float32)


def z_group(off):
    return [(off, i) for i in range(NX)]


def x_group(off):
    return [(i, off) for i in range(NZ)]


ROWS = 256
VMEM = pl.BlockSpec(memory_space=pltpu.VMEM)
SMEM = pl.BlockSpec(memory_space=pltpu.SMEM)


def own_keys_kernel(dev_ref, hbm_ref, a_low, a_high, b_low, b_high, out_ref, sum_ref, x_ref, sems):
    steps = hbm_ref.shape[0] // ROWS
    copies = []
    for i in range(steps):
        rows = pl.ds(i * ROWS, ROWS)
        copies.append(pltpu.make_async_copy(hbm_ref.at[rows], x_ref.at[rows], sems.at[i]))
        copies[i].start()
    for i in range(steps):
        rows = pl.ds(i * ROWS, ROWS)
        copies[i].wait()
        out_ref[rows, :512] = times(columns(x_ref, rows, dev_ref, z_group(0)), a_low, a_high)
        out_ref[rows, 512:] = times(columns(x_ref, rows, dev_ref, x_group(0)), b_low, b_high)
        x = x_ref[rows, :].astype(jnp.float32)
        sum_ref[rows, :] = jnp.broadcast_to(jnp.sum(x * x, axis=1, keepdims=True), (ROWS, 128))


def near_keys_kernel(dev_ref, x_ref, acc_ref, a1l, a1h, a3l, a3h, b1l, b1h, b3l, b3h, out_ref):
    def step(i, carry):
        rows = pl.ds(pl.multiple_of(i * ROWS, ROWS), ROWS)
        first = acc_ref[rows, :512]
        first += times(columns(x_ref, rows, dev_ref, z_group(1)), a1l, a1h)
        first += times(columns(x_ref, rows, dev_ref, z_group(3)), a3l, a3h)
        out_ref[rows, :512] = first
        second = acc_ref[rows, 512:]
        second += times(columns(x_ref, rows, dev_ref, x_group(1)), b1l, b1h)
        second += times(columns(x_ref, rows, dev_ref, x_group(3)), b3l, b3h)
        out_ref[rows, 512:] = second
        return carry

    lax.fori_loop(0, x_ref.shape[0] // ROWS, step, 0)


def own_keys(dev, tokens, parts):
    rows = tokens.shape[0]
    return pl.pallas_call(
        own_keys_kernel,
        out_shape=(
            jax.ShapeDtypeStruct((rows, 1024), jnp.float32),
            jax.ShapeDtypeStruct((rows, 128), jnp.float32),
            jax.ShapeDtypeStruct(tokens.shape, tokens.dtype),
        ),
        in_specs=[SMEM, pl.BlockSpec(memory_space=pltpu.HBM)] + [VMEM] * 4,
        out_specs=(VMEM, VMEM, VMEM),
        scratch_shapes=[pltpu.SemaphoreType.DMA((rows // ROWS,))],
        compiler_params=pltpu.CompilerParams(vmem_limit_bytes=OWN_LIMIT),
        name="own_keys",
    )(dev, pltpu.with_memory_space_constraint(tokens, pltpu.HBM), *parts)


def near_keys(dev, tokens, acc, parts):
    return pl.pallas_call(
        near_keys_kernel,
        out_shape=jax.ShapeDtypeStruct(acc.shape, jnp.float32),
        in_specs=[SMEM] + [VMEM] * 10,
        out_specs=VMEM,
        input_output_aliases={2: 0},
        compiler_params=pltpu.CompilerParams(vmem_limit_bytes=NEAR_LIMIT),
        name="near_keys",
    )(dev, tokens, acc, *parts)


def attend_kernel(
    dev_ref,
    len_ref,
    x_ref,
    acc_ref,
    sum_ref,
    a_low,
    a_high,
    b_low,
    b_high,
    q_ref,
    cos_ref,
    sin_ref,
    out_ref,
):
    width = x_ref.shape[1]
    heads = q_ref.shape[0] * 2
    per_key = heads // KV_HEADS
    cosine = cos_ref[...]
    sine = sin_ref[...]
    q = q_ref[:, :2, :].reshape(heads, HEAD_DIM)
    chosen = []
    for c in range(2):
        rows = pl.ds(c * LEN, LEN)
        halves = (
            acc_ref[rows, :512] + times(columns(x_ref, rows, dev_ref, z_group(2)), a_low, a_high),
            acc_ref[rows, 512:] + times(columns(x_ref, rows, dev_ref, x_group(2)), b_low, b_high),
        )
        parts = []
        for k in range(KV_HEADS):
            at = (k % 4) * 128
            key = halves[k // 4][:, at : at + 128]
            key = (key * cosine + pltpu.roll(key, 64, 1) * sine).astype(jnp.bfloat16)
            one = lax.dot_general(
                q, key, (((1,), (1,)), ((), ())), preferred_element_type=jnp.float32
            )
            parts.append(one[k * per_key : (k + 1) * per_key])
        scale = lax.rsqrt(jnp.transpose(sum_ref[rows, :])[:1] * (1.0 / width) + EPS)
        scores = jnp.concatenate(parts, axis=0) * scale * HEAD_DIM ** (-0.5)
        slot = lax.broadcasted_iota(jnp.int32, (heads, LEN), 1)
        scores = jnp.where(slot < len_ref[2 * dev_ref[3] + c], scores, -1e30)
        expo = jnp.exp(scores - jnp.max(scores, axis=1, keepdims=True))
        probs = expo / jnp.sum(expo, axis=1, keepdims=True) * scale
        mine = lax.rem(lax.broadcasted_iota(jnp.int32, (heads, LEN), 0), 2) == c
        chosen.append(jnp.where(mine, probs, 0.0).astype(jnp.bfloat16))
    probs = jnp.concatenate(chosen, axis=1)
    for i in range(4):
        at = slice(i * 1024, (i + 1) * 1024)
        pooled = jnp.dot(probs, x_ref[:, at], preferred_element_type=jnp.float32)
        out_ref[:, :, at] = pooled.astype(jnp.bfloat16).reshape(heads // 2, 2, 1024)


def attend(dev, lengths, tokens, acc, sums, far, exchange, cosine, sine):
    peers = exchange.shape[0]
    queries = pl.BlockSpec((peers, 16, HEAD_DIM), lambda i: (0, HEAD_DIM // 16, 0))
    return pl.pallas_call(
        attend_kernel,
        out_shape=jax.ShapeDtypeStruct((peers, 2, tokens.shape[1]), jnp.bfloat16),
        grid=(1,),
        in_specs=[SMEM, SMEM] + [VMEM] * 7 + [queries, VMEM, VMEM],
        out_specs=VMEM,
        compiler_params=pltpu.CompilerParams(vmem_limit_bytes=ATTEND_LIMIT),
        name="attend",
    )(dev, lengths, tokens, acc, sums, *far, exchange, cosine, sine)


def mix_kernel(x_ref, value_ref, out_w_ref, out_ref):
    peers, two, width = x_ref.shape
    pooled = x_ref[...].reshape(peers * two, width)
    values = value_ref[...].reshape(width, HEAD_DIM)
    mixed = jnp.dot(pooled, values, preferred_element_type=jnp.float32).astype(jnp.bfloat16)
    attn = jnp.dot(mixed, out_w_ref[...], preferred_element_type=jnp.float32)
    out_ref[...] = attn.astype(jnp.bfloat16).reshape(out_ref.shape)


def mix(pooled, exchange, w_out):
    peers = exchange.shape[0]
    values = pl.BlockSpec((peers, HEAD_DIM, HEAD_DIM), lambda i: (0, 0, 0))
    return pl.pallas_call(
        mix_kernel,
        out_shape=jax.ShapeDtypeStruct(pooled.shape, jnp.bfloat16),
        grid=(1,),
        in_specs=[VMEM, values, VMEM],
        out_specs=VMEM,
        compiler_params=pltpu.CompilerParams(vmem_limit_bytes=SMALL_LIMIT),
        name="mix",
    )(pooled, exchange, w_out)


def total(parts_ref):
    out = parts_ref[0].astype(jnp.float32)
    for i in range(1, parts_ref.shape[0]):
        out = out + parts_ref[i].astype(jnp.float32)
    return out


def middle_kernel(parts_ref, own_ref, gain_ref, out_ref, after_ref):
    after = own_ref[...] + total(parts_ref)
    after_ref[...] = after
    normed = (after * row_scale(after) * gain_ref[...]).astype(jnp.bfloat16)
    out_ref[...] = jnp.broadcast_to(normed[None], out_ref.shape)


def middle(parts, own_last, gain):
    return pl.pallas_call(
        middle_kernel,
        out_shape=(
            jax.ShapeDtypeStruct(parts.shape, jnp.bfloat16),
            jax.ShapeDtypeStruct(own_last.shape, jnp.float32),
        ),
        in_specs=[VMEM] * 3,
        out_specs=(VMEM, VMEM),
        compiler_params=pltpu.CompilerParams(vmem_limit_bytes=SMALL_LIMIT),
        name="middle",
    )(parts, own_last, gain)


def mlp_kernel(x_ref, gate_ref, up_ref, down_ref, out_ref):
    peers, two, width = x_ref.shape
    x = x_ref[...].reshape(peers * two, width)
    dims = (((1,), (1,)), ((), ()))
    gate = lax.dot_general(gate_ref[...], x, dims, preferred_element_type=jnp.float32)
    up = lax.dot_general(up_ref[...], x, dims, preferred_element_type=jnp.float32)
    act = jnp.transpose(gate / (1.0 + jnp.exp(-gate)) * up).astype(jnp.bfloat16)
    down = jnp.dot(act, down_ref[...], preferred_element_type=jnp.float32)
    out_ref[...] = down.astype(jnp.bfloat16).reshape(out_ref.shape)


def mlp(x, w_gate, w_up, w_down):
    return pl.pallas_call(
        mlp_kernel,
        out_shape=jax.ShapeDtypeStruct(x.shape, jnp.bfloat16),
        in_specs=[VMEM] * 4,
        out_specs=VMEM,
        compiler_params=pltpu.CompilerParams(vmem_limit_bytes=SMALL_LIMIT),
        name="mlp",
    )(x, w_gate, w_up, w_down)


def finish_kernel(parts_ref, after_ref, gain_ref, head_ref, out_ref):
    after = after_ref[...] + total(parts_ref)
    features = after * row_scale(after) * gain_ref[...]
    score = jnp.sum(features * head_ref[...], axis=1, keepdims=True)
    lane = lax.broadcasted_iota(jnp.int32, (1, 128), 1)
    tail = jnp.where(lane == 0, score[:1], jnp.where(lane == 1, score[1:], 0.0))
    peers = parts_ref.shape[0]
    for d in range(peers):
        cols = slice(d * 128, (d + 1) * 128)
        line = jnp.concatenate([features[:1, cols], features[1:, cols], tail], axis=1)
        for j in range(out_ref.shape[0] // peers):
            out_ref[j * peers + d] = line


def finish(parts, after_attn, gain, reward, devices):
    return pl.pallas_call(
        finish_kernel,
        out_shape=jax.ShapeDtypeStruct((devices, 1, 384), jnp.float32),
        in_specs=[VMEM] * 4,
        out_specs=VMEM,
        compiler_params=pltpu.CompilerParams(vmem_limit_bytes=SMALL_LIMIT),
        name="finish",
    )(parts, after_attn, gain, reward)


def remaining_candidates(judge_panel, duplicate_group_index, duplicate_groups):
    same = duplicate_group_index[:, None] == duplicate_group_index[None, :]
    top = jnp.max(jnp.where(same, judge_panel[None, :], -1e30), axis=1)
    expo = jnp.exp(judge_panel - top)
    total = jnp.sum(jnp.where(same, expo[None, :], 0.0), axis=1)
    weight_values = expo / total
    panel_member = (
        duplicate_group_index[:, None] == jnp.arange(duplicate_groups, dtype=jnp.int32)[None, :]
    ).astype(jnp.float32)
    return (weight_values, panel_member)


def layer(
    hidden,
    lengths,
    duplicate_group_index,
    attn_gain,
    w_query,
    w_key,
    w_value,
    w_out,
    mlp_gain,
    w_gate,
    w_up,
    w_down,
    final_gain,
    reward_head,
):
    judges = lax.axis_size("judge")
    devices = lax.axis_size("fsdp")
    me = lax.axis_index("fsdp")
    dev = jnp.stack([me // (NX * NZ), (me // NZ) % NX, me % NZ, me]).astype(jnp.int32)
    key_cos, key_sin = angles(jnp.arange(LEN, dtype=jnp.float32))
    tables = (
        jnp.concatenate([key_cos, key_cos], axis=1),
        jnp.concatenate([-key_sin, key_sin], axis=1),
    )
    tokens = hidden[0]
    tok_dev, width = tokens.shape
    seq_dev = tok_dev // LEN
    cands = lengths.shape[0]
    assert devices == GROUP and seq_dev == 2
    duplicate_groups = cands // 4

    row_gain = attn_gain[0].astype(jnp.float32)[:, None]
    key_rows = (w_key[0].astype(jnp.float32) * row_gain).astype(jnp.bfloat16)
    other = moved(key_rows, dy=1)
    both = jnp.concatenate([key_rows, other])
    line_x = small_ring(both[:, :512], "dx")
    line_z = small_ring(both[:, 512:], "dz")
    near_z, far_z = large_ring(*line_x, "dz")
    near_x, far_x = large_ring(*line_z, "dx")

    packed, own_last = pack_last(
        me[None], lengths, tokens, attn_gain, mlp_gain, final_gain, devices
    )
    shared = exchanged(packed, "fsdp")
    x_last = shared[:, :, :width].reshape(cands, width).astype(jnp.float32)
    gain_attn = shared[:, 0, width : width + 128].reshape(1, width).astype(jnp.float32)
    gain_final = shared[:, 0, width + 128 :].reshape(1, width).astype(jnp.float32)
    gain_mlp = shared[:, 1, width : width + 128].reshape(1, width).astype(jnp.float32)

    q_norm = (x_last * row_scale(x_last) * gain_attn).astype(jnp.bfloat16)
    q_part = jnp.dot(q_norm, w_query[0], preferred_element_type=jnp.float32)
    cosine, sine = angles((lengths - 1).astype(jnp.float32))
    q_part = rotate(q_part, cosine, sine).astype(jnp.bfloat16)
    value_rows = (w_value[0].astype(jnp.float32) * row_gain).astype(jnp.bfloat16)
    value_cols = jnp.swapaxes(value_rows.reshape(128, KV_HEADS, HEAD_DIM), 0, 1)
    value_cols = jnp.repeat(value_cols, devices // KV_HEADS, axis=0)
    q_part = jnp.pad(q_part.reshape(devices, seq_dev, HEAD_DIM), ((0, 0), (0, 14), (0, 0)))
    parcel = jnp.concatenate([value_cols, q_part], axis=1)
    both = exchanged(parcel, "fsdp")
    acc, sums, near_tokens = own_keys(dev, tokens, (*line_x, *line_z))
    acc = near_keys(dev, near_tokens, acc, (*near_z, *near_x))
    pooled = attend(
        dev,
        lengths,
        near_tokens,
        acc,
        sums,
        (*far_z, *far_x),
        both,
        *tables,
    )
    pooled = exchanged(pooled, "fsdp")
    attn = mix(pooled, both, w_out[0])
    attn = exchanged(attn, "fsdp")
    m_norm, after_attn = middle(attn, own_last, gain_mlp)
    m_norm = exchanged(m_norm, "fsdp")
    down = mlp(m_norm, w_gate[0].T, w_up[0].T, w_down[0])
    down = exchanged(down, "fsdp")

    cols = finish(down, after_attn, gain_final, reward_head, judges * devices)
    cols = exchanged(cols, ("judge", "fsdp"))
    mean = jnp.sum(cols.reshape(judges, devices, 384), axis=0) / judges
    total_cols = mean[:, :256].reshape(cands, 128)
    panel = mean[:, 256 : 256 + seq_dev].reshape(cands)
    weight_values, panel_member = remaining_candidates(
        panel, duplicate_group_index, duplicate_groups
    )
    cluster_cols = jnp.dot(
        panel_member.T, weight_values[:, None] * total_cols, precision=lax.Precision.HIGHEST
    )
    return (weight_values, cluster_cols)


def solution(mesh):
    in_specs = (
        P("judge", "fsdp", None),
        P(),
        P(),
        P("judge", "fsdp"),
        P("judge", None, "fsdp"),
        P("judge", "fsdp", None),
        P("judge", "fsdp", None),
        P("judge", "fsdp", None),
        P("judge", "fsdp"),
        P("judge", None, "fsdp"),
        P("judge", None, "fsdp"),
        P("judge", "fsdp", None),
        P("judge", "fsdp"),
        P("judge", None),
    )
    out_specs = (P(), P(None, "fsdp"))
    return jax.shard_map(layer, mesh=mesh, in_specs=in_specs, out_specs=out_specs, check_vma=False)
```

time: 387 us -> 210 us (0.54)
  waiting for transfers between devices: 102 us -> 35.1 us
  blocking collectives: 145 us -> 78.5 us
  matrix products: 42.3 us -> 1.19 us
  Pallas kernels: 0 us -> 29.6 us
  local copies, waits for them, and re-layouts: 35.3 us -> 12.5 us
  starting transfers between devices: 17.9 us -> 39.6 us
  other arithmetic: 29.1 us -> 11.4 us
  between operations: 14.4 us -> 1.14 us
    all_gather x1 -> x0, blocking collectives: 93.5 us -> none  [gather_packed(): lines, at, done = (lax.all_gather(ravelled, axis), 0, [])]
    all_gather x1 -> x0, waiting for transfers between devices: 77 us -> none  [sent_together(): filled, at, done = (lax.all_gather(both, axis, axis=dim, tiled=True), 0, [])]
    dot_general x9 -> x2, matrix products: 40.5 us -> 1.19 us  [the longest x1 0.87 us: layer(): jnp.dot(panel_member.T, weight_values[:, None] * total_cols, precision=la...]
    ppermute x0 -> x19, waiting for transfers between devices: none -> 35.1 us  [moved(): return lax.ppermute(v, 'fsdp', pairs)]
    pallas_call x0 -> x8, Pallas kernels: none -> 29.6 us  [the longest x1 9.06 us: near_keys(): pl.pallas_call(near_keys_kernel, out_shape=jax.ShapeDtypeStruct(acc.shape...]
    all_to_all x4 -> x5, blocking collectives: 51.1 us -> 78.5 us  [exchanged(): return lax.all_to_all(x, axis, 0, 0, tiled=True)]
    ppermute x0 -> x19, starting transfers between devices: none -> 26 us  [moved(): return lax.ppermute(v, 'fsdp', pairs)]
    all_to_all x3 -> x2, waiting for transfers between devices: 24.9 us -> 0.01 us  [exchanged(): return lax.all_to_all(x, axis, 0, 0, tiled=True)]
  transfers between devices with their start and end apart: 4 -> 21, of which waited for: 3 -> 4; matrix products, arithmetic and copies ran while one was open for 9% -> 5% of each run, Pallas kernels for 0% -> 9%
where the time goes in v1:
time: 210 us; the launch traced here: 209 us
  blocking collectives  78.5 us (37%)
  starting transfers between devices  39.6 us (19%)
  waiting for transfers between devices  35.1 us (17%)
  Pallas kernels  29.6 us (14%)
  local copies, waits for them, and re-layouts  12.5 us (6%)
  other arithmetic  11.4 us (5%)
    all_to_all x5, blocking collectives, exchanged(): return lax.all_to_all(x, axis, 0, 0, tiled=True)  78.5 us
    ppermute x19, waiting for transfers between devices, moved(): return lax.ppermute(v, 'fsdp', pairs)  35.1 us
    ppermute x19, starting transfers between devices, moved(): return lax.ppermute(v, 'fsdp', pairs)  26 us
    all_to_all x2, starting transfers between devices, exchanged(): return lax.all_to_all(x, axis, 0, 0, tiled=True)  13.6 us
    unnamed x58, local copies, waits for them, and re-layouts  11.9 us
    pallas_call x1, Pallas kernels, near_keys(): pl.pallas_call(near_keys_kernel, out_shape=jax.ShapeDtypeStruct(acc.shape...  9.06 us
    pallas_call x1, Pallas kernels, own_keys(): pl.pallas_call(own_keys_kernel, out_shape=(jax.ShapeDtypeStruct((rows, 10...  7.03 us
    pallas_call x1, Pallas kernels, attend(): pl.pallas_call(attend_kernel, out_shape=jax.ShapeDtypeStruct((peers, 2, t...  6.69 us
  transfers between devices with their start and end apart: 21, of which 4 were waited for; matrix products, arithmetic and copies ran while one was open for 5% of the time, Pallas kernels for 9%

profile of v1, /device:TPU:1, one launch (start us, length us, event | category | flops | bytes accessed | tf_op | source)
XLA Modules:
  0.0 209.0 jit_solution(17234197228926968615)
XLA Ops:
  0.6 0.7 bitcast_convert_fusion
  1.4 1.1 fusion.6
  2.5 2.2 %collective-permute-start = (bf16[128,1024]{1,0:T(8,128)(2,1)S(1)}, bf16[128,1024]{1,0:T(8,128)(2,1)S(1)}, u32[]{:S(2)}, u32[]{:S(2)}) collective-permute-start(bf16[128,1024]{1,0:T(8,128)(2,1)S(1)} %fusion.6), channel_id=1, source_target_pairs={{0,16},{1,17},{2,18},{3,19},{4,20},{5,21},{6,22},{7,23},{8,24},{9,... | collective-permute-start | bytes 786440 | tf_op jit(solution)/shard_map/ppermute | solution.py:37
  4.7 2.8 %pack_last.1 = (bf16[32,2,4352]{2,1,0:T(2,128)(2,1)}, f32[2,4096]{1,0:T(2,128)}) custom-call(s32[1]{0:T(128)} %bitcast.3.dev_ref, s32[64]{0:T(128)} %len_ref.3, bf16[1024,4096]{1,0:T(8,128)(2,1)} %bitcast.58, bf16[1024,4096]{1,0:T(8,128)(2,1)} %bitcast.59, bf16[1,128]{1,0:T(2,128)(2,1)} %ga_ref.1, bf16[1,128]{1,0:T(2,128)(2,1)} %gm_ref.1, bf16[1,128]{1,0:T(2,128)(2,1)} %gf_ref.1), custom_call_target="tpu_custom_call" | custom-call | tf_op jit(solution)/shard_map/pack_last/pallas_call | solution.py:117
  7.4 8.0 %all-to-all-start = ((bf16[32,2,4352]{2,1,0:T(2,128)(2,1)}), bf16[32,2,4352]{2,1,0:T(2,128)(2,1)S(1)}, u32[]{:S(2)}, u32[]{:S(2)}) async-start(bf16[32,2,4352]{2,1,0:T(2,128)(2,1)} %get-tuple-element.12), calls=%async_computation | async-start | bytes 1114112 | tf_op jit(solution)/shard_map/all_to_all | solution.py:61
  15.5 0.1 copy.21
  15.6 0.2 fusion.5
  15.8 0.8 pad_maximum_fusion.5
  16.6 2.7 %collective-permute-start.5 = (bf16[256,512]{1,0:T(8,128)(2,1)S(1)}, bf16[256,512]{1,0:T(8,128)(2,1)S(1)}, u32[]{:S(2)}, u32[]{:S(2)}) collective-permute-start(bf16[256,512]{1,0:T(8,128)(2,1)S(1)} %get-tuple-element.19), channel_id=1, source_target_pairs={{0,2},{1,3},{2,0},{3,1},{4,6},{5,7},{6,4},{7,5},{8,10},{9,11},{10,... | collective-permute-start | bytes 786440 | tf_op jit(solution)/shard_map/ppermute | solution.py:37
  19.3 0.3 collective-permute-start.6
  19.6 2.4 %collective-permute-start.4 = (bf16[256,512]{1,0:T(8,128)(2,1)S(1)}, bf16[256,512]{1,0:T(8,128)(2,1)S(1)}, u32[]{:S(2)}, u32[]{:S(2)}) collective-permute-start(bf16[256,512]{1,0:T(8,128)(2,1)S(1)} %get-tuple-element.19), channel_id=1, source_target_pairs={{0,3},{1,0},{2,1},{3,2},{4,7},{5,4},{6,5},{7,6},{8,11},{9,8},{10,9... | collective-permute-start | bytes 786440 | tf_op jit(solution)/shard_map/ppermute | solution.py:37
  22.0 1.2 collective-permute-start.3
  23.2 2.4 %collective-permute-start.2 = (bf16[256,512]{1,0:T(8,128)(2,1)}, bf16[256,512]{1,0:T(8,128)(2,1)S(1)}, u32[]{:S(2)}, u32[]{:S(2)}) collective-permute-start(bf16[256,512]{1,0:T(8,128)(2,1)} %get-tuple-element.20), channel_id=1, source_target_pairs={{0,8},{1,9},{2,10},{3,11},{4,12},{5,13},{6,14},{7,15},{8,0},{9,1},... | collective-permute-start | bytes 786440 | tf_op jit(solution)/shard_map/ppermute | solution.py:37
  25.6 5.4 %collective-permute-done.5 = bf16[256,512]{1,0:T(8,128)(2,1)S(1)} collective-permute-done((bf16[256,512]{1,0:T(8,128)(2,1)S(1)}, bf16[256,512]{1,0:T(8,128)(2,1)S(1)}, u32[]{:S(2)}, u32[]{:S(2)}) %collective-permute-start.5) | collective-permute-done | bytes 262176 | tf_op jit(solution)/shard_map/ppermute | solution.py:37
  31.1 2.7 %collective-permute-start.1 = (bf16[256,512]{1,0:T(8,128)(2,1)}, bf16[256,512]{1,0:T(8,128)(2,1)}, u32[]{:S(2)}, u32[]{:S(2)}) collective-permute-start(bf16[256,512]{1,0:T(8,128)(2,1)} %get-tuple-element.20), channel_id=1, source_target_pairs={{0,12},{1,13},{2,14},{3,15},{4,0},{5,1},{6,2},{7,3},{8,4},{9,5},{1... | collective-permute-start | bytes 786440 | tf_op jit(solution)/shard_map/ppermute | solution.py:37
  33.7 3.6 %collective-permute-done.6 = bf16[256,512]{1,0:T(8,128)(2,1)S(1)} collective-permute-done((bf16[256,512]{1,0:T(8,128)(2,1)S(1)}, bf16[256,512]{1,0:T(8,128)(2,1)S(1)}, u32[]{:S(2)}, u32[]{:S(2)}) %collective-permute-start.6) | collective-permute-done | bytes 262176 | tf_op jit(solution)/shard_map/ppermute | solution.py:37
  37.4 1.8 collective-permute-start.12
  39.4 0.9 pad_maximum_fusion.2.a_high
  40.3 0.5 collective-permute-start.8
  40.8 0.6 fusion
  41.4 0.6 fusion.26
  42.0 0.7 fusion.2
  42.7 0.2 convert_element_type.82
  42.9 0.3 fusion.3
  43.2 0.2 fusion.21
  43.5 0.2 broadcast_in_dim.36
  43.8 1.1 pad_maximum_fusion
  44.9 5.6 %all-to-all-start.1 = ((bf16[32,144,128]{2,1,0:T(8,128)(2,1)}), bf16[32,144,128]{2,1,0:T(8,128)(2,1)S(1)}, u32[]{:S(2)}, u32[]{:S(2)}) async-start(bf16[32,144,128]{2,1,0:T(8,128)(2,1)} %pad_maximum_fusion), calls=%async_computation.1 | async-start | bytes 2359296 | tf_op jit(solution)/shard_map/all_to_all | solution.py:61
  50.5 1.9 pad_maximum_fusion.1.a_low
  52.4 1.2 collective-permute-start.9
  53.6 1.2 collective-permute-start.14
  54.8 1.5 collective-permute-start.11
  56.3 1.2 collective-permute-start.10
  57.5 1.5 collective-permute-start.7
  59.0 19.6 %collective-permute-done.9.a3l = bf16[2,256,512]{2,1,0:T(8,128)(2,1)} collective-permute-done((bf16[2,256,512]{2,1,0:T(8,128)(2,1)}, bf16[2,256,512]{2,1,0:T(8,128)(2,1)}, u32[]{:S(2)}, u32[]{:S(2)}) %collective-permute-start.9) | collective-permute-done | bytes 524320 | tf_op jit(solution)/shard_map/ppermute | solution.py:37
  78.5 2.0 collective-permute-start.18
  80.6 0.8 copy-done.10
  81.4 0.8 copy-done.12
  82.2 1.2 collective-permute-start.16
  83.4 6.4 %collective-permute-done.10.a3h = bf16[2,256,512]{2,1,0:T(8,128)(2,1)S(1)} collective-permute-done((bf16[2,256,512]{2,1,0:T(8,128)(2,1)}, bf16[2,256,512]{2,1,0:T(8,128)(2,1)S(1)}, u32[]{:S(2)}, u32[]{:S(2)}) %collective-permute-start.10) | collective-permute-done | bytes 524320 | tf_op jit(solution)/shard_map/ppermute | solution.py:37
  89.8 0.8 copy-done.14
  90.7 1.0 fusion.13
  91.7 0.9 pad_maximum_fusion.6
  92.6 7.0 %own_keys.1 = (f32[1024,1024]{1,0:T(8,128)S(1)}, f32[1024,128]{1,0:T(8,128)S(1)}, bf16[1024,4096]{1,0:T(8,128)(2,1)S(1)}) custom-call(s32[4]{0:T(128)S(1)} %pad_add_fusion.dev_ref, bf16[1024,4096]{1,0:T(8,128)(2,1)} %bitcast.60, bf16[2,256,512]{2,1,0:T(8,128)(2,1)} %pad_maximum_fusion.1.a_low, bf16[2,256,512]{2,1,0:T(8,128)(2,1)} %pad_maximum_fusion.2.a_high, ...), custom_call_target="tpu_custom_call" | custom-call | tf_op jit(solution)/shard_map/own_keys/pallas_call | solution.py:198
  99.7 9.1 %near_keys.1.acc_ref = f32[1024,1024]{1,0:T(8,128)S(1)} custom-call(s32[4]{0:T(128)S(1)} %pad_add_fusion.dev_ref, bf16[1024,4096]{1,0:T(8,128)(2,1)S(1)} %get-tuple-element.9.x_ref, f32[1024,1024]{1,0:T(8,128)S(1)} %get-tuple-element.10.acc_ref, bf16[2,256,512]{2,1,0:T(8,128)(2,1)} %collective-permute-done.7.a1l, ...), custom_call_target="tpu_custom_call", output_to_operand_aliasing={{}: (2, {})} | custom-call | tf_op jit(solution)/shard_map/near_keys/pallas_call | solution.py:214
  108.8 2.0 copy-done.3
  110.9 3.4 %copy-done.2 = bf16[1024,4096]{1,0:T(8,128)(2,1)S(1)} copy-done((bf16[1024,4096]{1,0:T(8,128)(2,1)S(1)}, bf16[1024,4096]{1,0:T(8,128)(2,1)}, u32[]{:S(2)}) %copy-start.2) | copy-done | bytes 8388632
  114.3 2.2 %copy-done.4 = f32[1024,1024]{1,0:T(8,128)S(1)} copy-done((f32[1024,1024]{1,0:T(8,128)S(1)}, f32[1024,1024]{1,0:T(8,128)}, u32[]{:S(2)}) %copy-start.4) | copy-done | bytes 4194328
  116.4 1.0 copy-done.17
  117.5 0.7 copy-done.22
  118.1 6.7 %attend.1 = bf16[32,2,4096]{2,1,0:T(2,128)(2,1)S(1)} custom-call(s32[4]{0:T(128)S(1)} %copy-done.22, s32[64]{0:T(128)S(1)} %copy-done.24, bf16[1024,4096]{1,0:T(8,128)(2,1)S(1)} %copy-done.2, f32[1024,1024]{1,0:T(8,128)S(1)} %copy-done.4, f32[1024,128]{1,0:T(8,128)S(1)} %copy-done.17, bf16[2,256,512]{2,1,0:T(8,128)(2,1)} %collective-permute-done.15.a_low, ...), custom_call_target="tpu_custom_call" | custom-call | tf_op jit(solution)/shard_map/attend/pallas_call | solution.py:280
  124.8 17.0 %all_to_all.35.x_ref = bf16[32,2,4096]{2,1,0:T(2,128)(2,1)S(1)} all-to-all(bf16[32,2,4096]{2,1,0:T(2,128)(2,1)S(1)} %attend.1), channel_id=1, replica_groups=mesh['judge'=4,'fsdp'=32] {'fsdp'}, dimensions={0} | all-to-all | bytes 1048576 | tf_op jit(solution)/shard_map/all_to_all | solution.py:61
  141.9 0.7 mix.1
  142.6 14.1 %all_to_all.36.parts_ref = bf16[32,2,4096]{2,1,0:T(2,128)(2,1)S(1)} all-to-all(bf16[32,2,4096]{2,1,0:T(2,128)(2,1)S(1)} %mix.1), channel_id=1, replica_groups=mesh['judge'=4,'fsdp'=32] {'fsdp'}, dimensions={0} | all-to-all | bytes 1048576 | tf_op jit(solution)/shard_map/all_to_all | solution.py:61
  156.7 0.3 middle.1
  157.0 13.3 %all_to_all.37.x_ref = bf16[32,2,4096]{2,1,0:T(2,128)(2,1)S(1)} all-to-all(bf16[32,2,4096]{2,1,0:T(2,128)(2,1)S(1)} %get-tuple-element.14), channel_id=1, replica_groups=mesh['judge'=4,'fsdp'=32] {'fsdp'}, dimensions={0} | all-to-all | bytes 1048576 | tf_op jit(solution)/shard_map/all_to_all | solution.py:61
  170.3 2.9 %mlp.1 = bf16[32,2,4096]{2,1,0:T(2,128)(2,1)S(1)} custom-call(bf16[32,2,4096]{2,1,0:T(2,128)(2,1)S(1)} %all_to_all.37.x_ref, bf16[448,4096]{1,0:T(8,128)(2,1)S(1)} %bitcast.54, bf16[448,4096]{1,0:T(8,128)(2,1)S(1)} %bitcast.55, bf16[448,4096]{1,0:T(8,128)(2,1)S(1)} %bitcast.56), custom_call_target="tpu_custom_call" | custom-call | tf_op jit(solution)/shard_map/mlp/pallas_call | solution.py:354
  173.2 12.8 %all_to_all.38.parts_ref = bf16[32,2,4096]{2,1,0:T(2,128)(2,1)S(1)} all-to-all(bf16[32,2,4096]{2,1,0:T(2,128)(2,1)S(1)} %mlp.1), channel_id=1, replica_groups=mesh['judge'=4,'fsdp'=32] {'fsdp'}, dimensions={0} | all-to-all | bytes 1048576 | tf_op jit(solution)/shard_map/all_to_all | solution.py:61
  186.0 0.3 finish.1
  186.3 21.2 %all_to_all.39 = f32[128,1,384]{2,1,0:T(1,128)S(1)} all-to-all(f32[128,1,384]{2,1,0:T(1,128)S(1)} %finish.1), channel_id=1, replica_groups=mesh['judge'=4,'fsdp'=32] {'judge','fsdp'}, dimensions={0} | all-to-all | bytes 393216 | tf_op jit(solution)/shard_map/all_to_all | solution.py:61
  207.7 0.1 reshape.129
  207.8 0.2 fusion.18
  208.0 0.2 fusion.19
  208.2 0.9 fusion.24
  (85 shorter events, 0.7 us)
Async XLA Ops:
  0.6 42.3 %copy-start = (bf16[1,4096,128]{2,1,0:T(8,128)(2,1)S(1)}, bf16[1,4096,128]{2,1,0:T(8,128)(2,1)}, u32[]{:S(2)}) copy-start(bf16[1,4096,128]{2,1,0:T(8,128)(2,1)} %param.18) | copy-start | bytes 3145732
  2.5 13.3 %collective-permute-start = (bf16[128,1024]{1,0:T(8,128)(2,1)S(1)}, bf16[128,1024]{1,0:T(8,128)(2,1)S(1)}, u32[]{:S(2)}, u32[]{:S(2)}) collective-permute-start(bf16[128,1024]{1,0:T(8,128)(2,1)S(1)} %fusion.6), channel_id=1, source_target_pairs={{0,16},{1,17},{2,18},{3,19},{4,20},{5,21},{6,22},{7,23},{8,24},{9,... | collective-permute-start | bytes 786440 | tf_op jit(solution)/shard_map/ppermute | solution.py:37
  4.7 10.8 %copy-start.25 = (bf16[1,128,1024]{2,1,0:T(8,128)(2,1)S(1)}, bf16[1,128,1024]{2,1,0:T(8,128)(2,1)}, u32[]{:S(2)}) copy-start(bf16[1,128,1024]{2,1,0:T(8,128)(2,1)} %param.20) | copy-start | bytes 786436
  7.4 14.6 %copy-start.23 = (s32[64]{0:T(128)S(1)}, s32[64]{0:T(128)}, u32[]{:S(2)}) copy-start(s32[64]{0:T(128)} %len_ref.3) | copy-start | bytes 772
  7.4 33.4 %all-to-all-start = ((bf16[32,2,4352]{2,1,0:T(2,128)(2,1)}), bf16[32,2,4352]{2,1,0:T(2,128)(2,1)S(1)}, u32[]{:S(2)}, u32[]{:S(2)}) async-start(bf16[32,2,4352]{2,1,0:T(2,128)(2,1)} %get-tuple-element.12), calls=%async_computation | async-start | bytes 1114112 | tf_op jit(solution)/shard_map/all_to_all | solution.py:61
  16.6 14.5 %collective-permute-start.5 = (bf16[256,512]{1,0:T(8,128)(2,1)S(1)}, bf16[256,512]{1,0:T(8,128)(2,1)S(1)}, u32[]{:S(2)}, u32[]{:S(2)}) collective-permute-start(bf16[256,512]{1,0:T(8,128)(2,1)S(1)} %get-tuple-element.19), channel_id=1, source_target_pairs={{0,2},{1,3},{2,0},{3,1},{4,6},{5,7},{6,4},{7,5},{8,10},{9,11},{10,... | collective-permute-start | bytes 786440 | tf_op jit(solution)/shard_map/ppermute | solution.py:37
  19.3 18.0 %collective-permute-start.6 = (bf16[256,512]{1,0:T(8,128)(2,1)S(1)}, bf16[256,512]{1,0:T(8,128)(2,1)S(1)}, u32[]{:S(2)}, u32[]{:S(2)}) collective-permute-start(bf16[256,512]{1,0:T(8,128)(2,1)S(1)} %get-tuple-element.19), channel_id=1, source_target_pairs={{0,1},{1,2},{2,3},{3,0},{4,5},{5,6},{6,7},{7,4},{8,9},{9,10},{10,1... | collective-permute-start | bytes 786440 | tf_op jit(solution)/shard_map/ppermute | solution.py:37
  19.6 19.7 %collective-permute-start.4 = (bf16[256,512]{1,0:T(8,128)(2,1)S(1)}, bf16[256,512]{1,0:T(8,128)(2,1)S(1)}, u32[]{:S(2)}, u32[]{:S(2)}) collective-permute-start(bf16[256,512]{1,0:T(8,128)(2,1)S(1)} %get-tuple-element.19), channel_id=1, source_target_pairs={{0,3},{1,0},{2,1},{3,2},{4,7},{5,4},{6,5},{7,6},{8,11},{9,8},{10,9... | collective-permute-start | bytes 786440 | tf_op jit(solution)/shard_map/ppermute | solution.py:37
  22.0 17.4 %collective-permute-start.3 = (bf16[256,512]{1,0:T(8,128)(2,1)}, bf16[256,512]{1,0:T(8,128)(2,1)S(1)}, u32[]{:S(2)}, u32[]{:S(2)}) collective-permute-start(bf16[256,512]{1,0:T(8,128)(2,1)} %get-tuple-element.20), channel_id=1, source_target_pairs={{0,4},{1,5},{2,6},{3,7},{4,8},{5,9},{6,10},{7,11},{8,12},{9,13},{1... | collective-permute-start | bytes 786440 | tf_op jit(solution)/shard_map/ppermute | solution.py:37
  23.2 16.2 %collective-permute-start.2 = (bf16[256,512]{1,0:T(8,128)(2,1)}, bf16[256,512]{1,0:T(8,128)(2,1)S(1)}, u32[]{:S(2)}, u32[]{:S(2)}) collective-permute-start(bf16[256,512]{1,0:T(8,128)(2,1)} %get-tuple-element.20), channel_id=1, source_target_pairs={{0,8},{1,9},{2,10},{3,11},{4,12},{5,13},{6,14},{7,15},{8,0},{9,1},... | collective-permute-start | bytes 786440 | tf_op jit(solution)/shard_map/ppermute | solution.py:37
  31.1 19.4 %collective-permute-start.1 = (bf16[256,512]{1,0:T(8,128)(2,1)}, bf16[256,512]{1,0:T(8,128)(2,1)}, u32[]{:S(2)}, u32[]{:S(2)}) collective-permute-start(bf16[256,512]{1,0:T(8,128)(2,1)} %get-tuple-element.20), channel_id=1, source_target_pairs={{0,12},{1,13},{2,14},{3,15},{4,0},{5,1},{6,2},{7,3},{8,4},{9,5},{1... | collective-permute-start | bytes 786440 | tf_op jit(solution)/shard_map/ppermute | solution.py:37
  37.4 17.4 %collective-permute-start.12 = (bf16[2,256,512]{2,1,0:T(8,128)(2,1)S(1)}, bf16[2,256,512]{2,1,0:T(8,128)(2,1)}, u32[]{:S(2)}, u32[]{:S(2)}) collective-permute-start(bf16[2,256,512]{2,1,0:T(8,128)(2,1)S(1)} %pad_maximum_fusion.4.b_high), channel_id=1, source_target_pairs={{0,12},{1,13},{2,14},{3,15},{4,0},{5,1},{6,2},{7,3},{8,4},{9,5},{1... | collective-permute-start | bytes 1572872 | tf_op jit(solution)/shard_map/ppermute | solution.py:37
  39.3 17.0 %collective-permute-start.13 = (bf16[2,256,512]{2,1,0:T(8,128)(2,1)S(1)}, bf16[2,256,512]{2,1,0:T(8,128)(2,1)}, u32[]{:S(2)}, u32[]{:S(2)}) collective-permute-start(bf16[2,256,512]{2,1,0:T(8,128)(2,1)S(1)} %pad_maximum_fusion.3.b_low), channel_id=1, source_target_pairs={{0,4},{1,5},{2,6},{3,7},{4,8},{5,9},{6,10},{7,11},{8,12},{9,13},{1... | collective-permute-start | bytes 1572872 | tf_op jit(solution)/shard_map/ppermute | solution.py:37
  40.3 17.2 %collective-permute-start.8 = (bf16[2,256,512]{2,1,0:T(8,128)(2,1)}, bf16[2,256,512]{2,1,0:T(8,128)(2,1)}, u32[]{:S(2)}, u32[]{:S(2)}) collective-permute-start(bf16[2,256,512]{2,1,0:T(8,128)(2,1)} %pad_maximum_fusion.2.a_high), channel_id=1, source_target_pairs={{0,3},{1,0},{2,1},{3,2},{4,7},{5,4},{6,5},{7,6},{8,11},{9,8},{10,9... | collective-permute-start | bytes 1572872 | tf_op jit(solution)/shard_map/ppermute | solution.py:37
  44.9 66.0 %all-to-all-start.1 = ((bf16[32,144,128]{2,1,0:T(8,128)(2,1)}), bf16[32,144,128]{2,1,0:T(8,128)(2,1)S(1)}, u32[]{:S(2)}, u32[]{:S(2)}) async-start(bf16[32,144,128]{2,1,0:T(8,128)(2,1)} %pad_maximum_fusion), calls=%async_computation.1 | async-start | bytes 2359296 | tf_op jit(solution)/shard_map/all_to_all | solution.py:61
  52.4 26.2 %collective-permute-start.9 = (bf16[2,256,512]{2,1,0:T(8,128)(2,1)}, bf16[2,256,512]{2,1,0:T(8,128)(2,1)}, u32[]{:S(2)}, u32[]{:S(2)}) collective-permute-start(bf16[2,256,512]{2,1,0:T(8,128)(2,1)} %pad_maximum_fusion.1.a_low), channel_id=1, source_target_pairs={{0,1},{1,2},{2,3},{3,0},{4,5},{5,6},{6,7},{7,4},{8,9},{9,10},{10,1... | collective-permute-start | bytes 1572872 | tf_op jit(solution)/shard_map/ppermute | solution.py:37
  53.6 27.0 %collective-permute-start.14 = (bf16[2,256,512]{2,1,0:T(8,128)(2,1)S(1)}, bf16[2,256,512]{2,1,0:T(8,128)(2,1)S(1)}, u32[]{:S(2)}, u32[]{:S(2)}) collective-permute-start(bf16[2,256,512]{2,1,0:T(8,128)(2,1)S(1)} %pad_maximum_fusion.4.b_high), channel_id=1, source_target_pairs={{0,4},{1,5},{2,6},{3,7},{4,8},{5,9},{6,10},{7,11},{8,12},{9,13},{1... | collective-permute-start | bytes 1572872 | tf_op jit(solution)/shard_map/ppermute | solution.py:37
  54.8 26.6 %collective-permute-start.11 = (bf16[2,256,512]{2,1,0:T(8,128)(2,1)S(1)}, bf16[2,256,512]{2,1,0:T(8,128)(2,1)S(1)}, u32[]{:S(2)}, u32[]{:S(2)}) collective-permute-start(bf16[2,256,512]{2,1,0:T(8,128)(2,1)S(1)} %pad_maximum_fusion.3.b_low), channel_id=1, source_target_pairs={{0,12},{1,13},{2,14},{3,15},{4,0},{5,1},{6,2},{7,3},{8,4},{9,5},{1... | collective-permute-start | bytes 1572872 | tf_op jit(solution)/shard_map/ppermute | solution.py:37
  56.3 33.5 %collective-permute-start.10 = (bf16[2,256,512]{2,1,0:T(8,128)(2,1)}, bf16[2,256,512]{2,1,0:T(8,128)(2,1)S(1)}, u32[]{:S(2)}, u32[]{:S(2)}) collective-permute-start(bf16[2,256,512]{2,1,0:T(8,128)(2,1)} %pad_maximum_fusion.2.a_high), channel_id=1, source_target_pairs={{0,1},{1,2},{2,3},{3,0},{4,5},{5,6},{6,7},{7,4},{8,9},{9,10},{10,1... | collective-permute-start | bytes 1572872 | tf_op jit(solution)/shard_map/ppermute | solution.py:37
  57.5 42.1 %collective-permute-start.7 = (bf16[2,256,512]{2,1,0:T(8,128)(2,1)}, bf16[2,256,512]{2,1,0:T(8,128)(2,1)}, u32[]{:S(2)}, u32[]{:S(2)}) collective-permute-start(bf16[2,256,512]{2,1,0:T(8,128)(2,1)} %pad_maximum_fusion.1.a_low), channel_id=1, source_target_pairs={{0,3},{1,0},{2,1},{3,2},{4,7},{5,4},{6,5},{7,6},{8,11},{9,8},{10,9... | collective-permute-start | bytes 1572872 | tf_op jit(solution)/shard_map/ppermute | solution.py:37
  78.5 32.3 %collective-permute-start.18 = (bf16[2,256,512]{2,1,0:T(8,128)(2,1)}, bf16[2,256,512]{2,1,0:T(8,128)(2,1)}, u32[]{:S(2)}, u32[]{:S(2)}) collective-permute-start(bf16[2,256,512]{2,1,0:T(8,128)(2,1)} %collective-permute-done.12.b1h), channel_id=1, source_target_pairs={{0,12},{1,13},{2,14},{3,15},{4,0},{5,1},{6,2},{7,3},{8,4},{9,5},{1... | collective-permute-start | bytes 1572872 | tf_op jit(solution)/shard_map/ppermute | solution.py:37
  80.6 0.8 copy-start.10
  81.4 29.4 %collective-permute-start.17 = (bf16[2,256,512]{2,1,0:T(8,128)(2,1)}, bf16[2,256,512]{2,1,0:T(8,128)(2,1)}, u32[]{:S(2)}, u32[]{:S(2)}) collective-permute-start(bf16[2,256,512]{2,1,0:T(8,128)(2,1)} %collective-permute-done.13.b3l), channel_id=1, source_target_pairs={{0,4},{1,5},{2,6},{3,7},{4,8},{5,9},{6,10},{7,11},{8,12},{9,13},{1... | collective-permute-start | bytes 1572872 | tf_op jit(solution)/shard_map/ppermute | solution.py:37
  81.4 0.8 copy-start.12
  82.2 28.6 %collective-permute-start.16 = (bf16[2,256,512]{2,1,0:T(8,128)(2,1)}, bf16[2,256,512]{2,1,0:T(8,128)(2,1)}, u32[]{:S(2)}, u32[]{:S(2)}) collective-permute-start(bf16[2,256,512]{2,1,0:T(8,128)(2,1)} %collective-permute-done.8.a1h), channel_id=1, source_target_pairs={{0,3},{1,0},{2,1},{3,2},{4,7},{5,4},{6,5},{7,6},{8,11},{9,8},{10,9... | collective-permute-start | bytes 1572872 | tf_op jit(solution)/shard_map/ppermute | solution.py:37
  89.8 0.8 copy-start.14
  90.6 20.2 %collective-permute-start.15 = (bf16[2,256,512]{2,1,0:T(8,128)(2,1)}, bf16[2,256,512]{2,1,0:T(8,128)(2,1)}, u32[]{:S(2)}, u32[]{:S(2)}) collective-permute-start(bf16[2,256,512]{2,1,0:T(8,128)(2,1)} %collective-permute-done.9.a3l), channel_id=1, source_target_pairs={{0,1},{1,2},{2,3},{3,0},{4,5},{5,6},{6,7},{7,4},{8,9},{9,10},{10,1... | collective-permute-start | bytes 1572872 | tf_op jit(solution)/shard_map/ppermute | solution.py:37
  90.7 9.0 %copy-start.21 = (s32[4]{0:T(128)}, s32[4]{0:T(128)S(1)}, u32[]{:S(2)}) copy-start(s32[4]{0:T(128)S(1)} %pad_add_fusion.dev_ref) | copy-start | bytes 52
  92.6 7.1 %copy-start.11 = (bf16[2,256,512]{2,1,0:T(8,128)(2,1)S(1)}, bf16[2,256,512]{2,1,0:T(8,128)(2,1)}, u32[]{:S(2)}) copy-start(bf16[2,256,512]{2,1,0:T(8,128)(2,1)} %copy-done.10) | copy-start | bytes 1572868
  92.6 7.1 %copy-start.13 = (bf16[2,256,512]{2,1,0:T(8,128)(2,1)S(1)}, bf16[2,256,512]{2,1,0:T(8,128)(2,1)}, u32[]{:S(2)}) copy-start(bf16[2,256,512]{2,1,0:T(8,128)(2,1)} %copy-done.12) | copy-start | bytes 1572868
  92.6 7.1 %copy-start.15 = (bf16[2,256,512]{2,1,0:T(8,128)(2,1)S(1)}, bf16[2,256,512]{2,1,0:T(8,128)(2,1)}, u32[]{:S(2)}) copy-start(bf16[2,256,512]{2,1,0:T(8,128)(2,1)} %copy-done.14) | copy-start | bytes 1572868
  99.6 9.2 %copy-start.1 = (bf16[1024,4096]{1,0:T(8,128)(2,1)}, bf16[1024,4096]{1,0:T(8,128)(2,1)S(1)}, u32[]{:S(2)}) copy-start(bf16[1024,4096]{1,0:T(8,128)(2,1)S(1)} %get-tuple-element.9.x_ref) | copy-start | bytes 25165828
  99.6 9.2 %copy-start.16 = (f32[1024,128]{1,0:T(8,128)}, f32[1024,128]{1,0:T(8,128)S(1)}, u32[]{:S(2)}) copy-start(f32[1024,128]{1,0:T(8,128)S(1)} %get-tuple-element.11.sum_ref) | copy-start | bytes 1572868
  99.7 11.2 %copy-start.8 = (f32[512,128]{1,0:T(8,128)S(1)}, f32[512,128]{1,0:T(8,128)}, u32[]{:S(2)}) copy-start(f32[512,128]{1,0:T(8,128)} %get-tuple-element.27.sin_ref) | copy-start | bytes 786436
  99.7 11.2 %copy-start.24 = (s32[64]{0:T(128)S(1)}, s32[64]{0:T(128)}, u32[]{:S(2)}) copy-start(s32[64]{0:T(128)} %len_ref.3) | copy-start | bytes 772
  108.8 2.0 copy-start.3
  110.9 3.4 %copy-start.2 = (bf16[1024,4096]{1,0:T(8,128)(2,1)S(1)}, bf16[1024,4096]{1,0:T(8,128)(2,1)}, u32[]{:S(2)}) copy-start(bf16[1024,4096]{1,0:T(8,128)(2,1)} %copy-done.1) | copy-start | bytes 25165828
  114.3 2.2 %copy-start.4 = (f32[1024,1024]{1,0:T(8,128)S(1)}, f32[1024,1024]{1,0:T(8,128)}, u32[]{:S(2)}) copy-start(f32[1024,1024]{1,0:T(8,128)} %copy-done.3) | copy-start | bytes 12582916
  116.4 1.0 copy-start.17
  117.5 0.7 copy-start.22
  118.1 23.7 %copy-start.9 = (bf16[1,128,4096]{2,1,0:T(8,128)(2,1)S(1)}, bf16[1,128,4096]{2,1,0:T(8,128)(2,1)}, u32[]{:S(2)}) copy-start(bf16[1,128,4096]{2,1,0:T(8,128)(2,1)} %param.21) | copy-start | bytes 3145732
  118.1 52.2 %copy-start.6 = (bf16[1,4096,448]{1,2,0:T(8,128)(2,1)S(1)}, bf16[1,4096,448]{1,2,0:T(8,128)(2,1)}, u32[]{:S(2)}) copy-start(bf16[1,4096,448]{1,2,0:T(8,128)(2,1)} %param.24) | copy-start | bytes 11010052
  118.1 52.2 %copy-start.7 = (bf16[1,448,4096]{2,1,0:T(8,128)(2,1)S(1)}, bf16[1,448,4096]{2,1,0:T(8,128)(2,1)}, u32[]{:S(2)}) copy-start(bf16[1,448,4096]{2,1,0:T(8,128)(2,1)} %param.25) | copy-start | bytes 11010052
  141.9 14.8 %copy-start.18 = (f32[1,4096]{1,0:T(1,128)S(1)}, f32[1,4096]{1,0:T(1,128)}, u32[]{:S(2)}) copy-start(f32[1,4096]{1,0:T(1,128)} %get-tuple-element.17.gain_ref) | copy-start | bytes 49156
  141.9 14.8 %copy-start.19 = (f32[2,4096]{1,0:T(2,128)S(1)}, f32[2,4096]{1,0:T(2,128)}, u32[]{:S(2)}) copy-start(f32[2,4096]{1,0:T(2,128)} %get-tuple-element.13.own_ref) | copy-start | bytes 98308
  141.9 28.4 %copy-start.5 = (bf16[1,4096,448]{1,2,0:T(8,128)(2,1)S(1)}, bf16[1,4096,448]{1,2,0:T(8,128)(2,1)}, u32[]{:S(2)}) copy-start(bf16[1,4096,448]{1,2,0:T(8,128)(2,1)} %param.23) | copy-start | bytes 11010052
  170.3 15.7 %copy-start.20 = (f32[1,4096]{1,0:T(1,128)S(1)}, f32[1,4096]{1,0:T(1,128)}, u32[]{:S(2)}) copy-start(f32[1,4096]{1,0:T(1,128)} %head_ref.1) | copy-start | bytes 49156
  173.2 34.6 %copy-start.26 = (s32[64]{0:T(128)S(1)}, s32[64]{0:T(128)}, u32[]{:S(2)}) copy-start(s32[64]{0:T(128)} %param.16) | copy-start | bytes 772
  208.2 0.9 copy-start.27

commit v2 on v1

--- a/solution.py
+++ b/solution.py
@@ -17,6 +17,9 @@
 GROUP = NY * NX * NZ
 
 
+ROWS = 256
+VMEM = pl.BlockSpec(memory_space=pltpu.VMEM)
+SMEM = pl.BlockSpec(memory_space=pltpu.SMEM)
 OWN_LIMIT = 16 << 20
 SMALL_LIMIT = 12 << 20
 NEAR_LIMIT = 16 << 20
@@ -72,12 +75,11 @@
     return (jnp.cos(turned), jnp.sin(turned))
 
 
-def rotate(v, cosine, sine):
-    half = HEAD_DIM // 2
-    first = v[..., :half]
-    second = v[..., half:]
-    return jnp.concatenate(
-        [first * cosine - second * sine, second * cosine + first * sine], axis=-1
+def turn_tables(position):
+    cosine, sine = angles(position)
+    return (
+        jnp.concatenate([cosine, cosine], axis=-1),
+        jnp.concatenate([-sine, sine], axis=-1),
     )
 
 
@@ -133,6 +135,47 @@
     )(dev, lengths, tokens, tokens, attn_gain, mlp_gain, final_gain)
 
 
+def parcel_kernel(
+    shared_ref, w_ref, cos_ref, sin_ref, value_ref, out_ref, mlp_ref, final_ref
+):
+    peers = shared_ref.shape[0]
+    width = w_ref.shape[0]
+
+    def gain(row, at):
+        lines = shared_ref[:, row, at : at + 128].astype(jnp.float32)
+        return jnp.concatenate([lines[d : d + 1] for d in range(peers)], axis=1)
+
+    mlp_ref[...] = gain(1, width)
+    final_ref[...] = gain(0, width + 128)
+    each = peers // KV_HEADS
+    for k in range(KV_HEADS):
+        for h in range(k * each, (k + 1) * each):
+            out_ref[h, :HEAD_DIM] = value_ref[k]
+    x = shared_ref[:, :, :width].reshape(2 * peers, width).astype(jnp.float32)
+    normed = (x * row_scale(x) * gain(0, width)).astype(jnp.bfloat16)
+    q = jnp.dot(normed, w_ref[...], preferred_element_type=jnp.float32)
+    q = (q * cos_ref[...] + pltpu.roll(q, 64, 1) * sin_ref[...]).reshape(peers, 2, HEAD_DIM)
+    q = jnp.concatenate([q, jnp.zeros((peers, 14, HEAD_DIM), jnp.float32)], axis=1)
+    out_ref[:, HEAD_DIM:] = q.astype(jnp.bfloat16)
+
+
+def make_parcel(shared, w_query, turns, value_cols):
+    peers = shared.shape[0]
+    width = w_query.shape[0]
+    return pl.pallas_call(
+        parcel_kernel,
+        out_shape=(
+            jax.ShapeDtypeStruct((peers, HEAD_DIM + 16, HEAD_DIM), jnp.bfloat16),
+            jax.ShapeDtypeStruct((1, width), jnp.float32),
+            jax.ShapeDtypeStruct((1, width), jnp.float32),
+        ),
+        in_specs=[VMEM] * 5,
+        out_specs=(VMEM,) * 3,
+        compiler_params=pltpu.CompilerParams(vmem_limit_bytes=SMALL_LIMIT),
+        name="parcel",
+    )(shared, w_query, *turns, value_cols)
+
+
 def columns(x_ref, rows, dev_ref, blocks):
     parts = []
     for zo, xo in blocks:
@@ -154,11 +197,6 @@
 
 def x_group(off):
     return [(i, off) for i in range(NZ)]
-
-
-ROWS = 256
-VMEM = pl.BlockSpec(memory_space=pltpu.VMEM)
-SMEM = pl.BlockSpec(memory_space=pltpu.SMEM)
 
 
 def own_keys_kernel(dev_ref, hbm_ref, a_low, a_high, b_low, b_high, out_ref, sum_ref, x_ref, sems):
@@ -418,46 +456,39 @@
     devices = lax.axis_size("fsdp")
     me = lax.axis_index("fsdp")
     dev = jnp.stack([me // (NX * NZ), (me // NZ) % NX, me % NZ, me]).astype(jnp.int32)
-    key_cos, key_sin = angles(jnp.arange(LEN, dtype=jnp.float32))
-    tables = (
-        jnp.concatenate([key_cos, key_cos], axis=1),
-        jnp.concatenate([-key_sin, key_sin], axis=1),
-    )
+    turns = turn_tables((lengths - 1).astype(jnp.float32))
     tokens = hidden[0]
-    tok_dev, width = tokens.shape
+    tok_dev, _ = tokens.shape
     seq_dev = tok_dev // LEN
     cands = lengths.shape[0]
     assert devices == GROUP and seq_dev == 2
     duplicate_groups = cands // 4
 
     row_gain = attn_gain[0].astype(jnp.float32)[:, None]
-    key_rows = (w_key[0].astype(jnp.float32) * row_gain).astype(jnp.bfloat16)
-    other = moved(key_rows, dy=1)
-    both = jnp.concatenate([key_rows, other])
+    other = moved(w_key[0], dy=1)
+    other_gain = moved(attn_gain[0], dy=1).astype(jnp.float32)[:, None]
+    both = jnp.concatenate(
+        [
+            (w_key[0].astype(jnp.float32) * row_gain).astype(jnp.bfloat16),
+            (other.astype(jnp.float32) * other_gain).astype(jnp.bfloat16),
+        ]
+    )
     line_x = small_ring(both[:, :512], "dx")
     line_z = small_ring(both[:, 512:], "dz")
     near_z, far_z = large_ring(*line_x, "dz")
     near_x, far_x = large_ring(*line_z, "dx")
 
+    tables = turn_tables(jnp.arange(LEN, dtype=jnp.float32))
+
     packed, own_last = pack_last(
         me[None], lengths, tokens, attn_gain, mlp_gain, final_gain, devices
     )
     shared = exchanged(packed, "fsdp")
-    x_last = shared[:, :, :width].reshape(cands, width).astype(jnp.float32)
-    gain_attn = shared[:, 0, width : width + 128].reshape(1, width).astype(jnp.float32)
-    gain_final = shared[:, 0, width + 128 :].reshape(1, width).astype(jnp.float32)
-    gain_mlp = shared[:, 1, width : width + 128].reshape(1, width).astype(jnp.float32)
-
-    q_norm = (x_last * row_scale(x_last) * gain_attn).astype(jnp.bfloat16)
-    q_part = jnp.dot(q_norm, w_query[0], preferred_element_type=jnp.float32)
-    cosine, sine = angles((lengths - 1).astype(jnp.float32))
-    q_part = rotate(q_part, cosine, sine).astype(jnp.bfloat16)
     value_rows = (w_value[0].astype(jnp.float32) * row_gain).astype(jnp.bfloat16)
     value_cols = jnp.swapaxes(value_rows.reshape(128, KV_HEADS, HEAD_DIM), 0, 1)
-    value_cols = jnp.repeat(value_cols, devices // KV_HEADS, axis=0)
-    q_part = jnp.pad(q_part.reshape(devices, seq_dev, HEAD_DIM), ((0, 0), (0, 14), (0, 0)))
-    parcel = jnp.concatenate([value_cols, q_part], axis=1)
+    parcel, gain_mlp, gain_final = make_parcel(shared, w_query[0], turns, value_cols)
     both = exchanged(parcel, "fsdp")
+
     acc, sums, near_tokens = own_keys(dev, tokens, (*line_x, *line_z))
     acc = near_keys(dev, near_tokens, acc, (*near_z, *near_x))
     pooled = attend(

time: 210 us -> 207 us (0.986)
  other arithmetic: 11.4 us -> 4.77 us
  local copies, waits for them, and re-layouts: 12.5 us -> 14.8 us
    unnamed x58 -> x68, local copies, waits for them, and re-layouts: 11.9 us -> 14.6 us
    convert_element_type x5 -> x4, other arithmetic: 2.56 us -> 0.23 us  [the longest x1 0.11 us: layer(): (other.astype(jnp.float32) * other_gain).astype(jnp.bfloat16)]
    ppermute x19 -> x20, waiting for transfers between devices: 35.1 us -> 35.5 us  [moved(): return lax.ppermute(v, 'fsdp', pairs)]
    ppermute x19 -> x20, starting transfers between devices: 26 us -> 26.2 us  [moved(): return lax.ppermute(v, 'fsdp', pairs)]
  transfers between devices with their start and end apart: 21 -> 22, of which waited for: 4 -> 4; matrix products, arithmetic and copies ran while one was open for 5% -> 2% of each run, Pallas kernels for 9% -> 9%
where the time goes in v2:
time: 207 us; the launch traced here: 206 us
  blocking collectives  78.5 us (38%)
  starting transfers between devices  41 us (20%)
  waiting for transfers between devices  35.5 us (17%)
  Pallas kernels  29.7 us (14%)
  local copies, waits for them, and re-layouts  14.8 us (7%)
  other arithmetic  4.77 us (2%)
    all_to_all x5, blocking collectives, exchanged(): return lax.all_to_all(x, axis, 0, 0, tiled=True)  78.5 us
    ppermute x20, waiting for transfers between devices, moved(): return lax.ppermute(v, 'fsdp', pairs)  35.5 us
    ppermute x20, starting transfers between devices, moved(): return lax.ppermute(v, 'fsdp', pairs)  26.2 us
    all_to_all x2, starting transfers between devices, exchanged(): return lax.all_to_all(x, axis, 0, 0, tiled=True)  14.8 us
    unnamed x68, local copies, waits for them, and re-layouts  14.6 us
    pallas_call x1, Pallas kernels, near_keys(): pl.pallas_call(near_keys_kernel, out_shape=jax.ShapeDtypeStruct(acc.shape...  9.08 us
    pallas_call x1, Pallas kernels, attend(): pl.pallas_call(attend_kernel, out_shape=jax.ShapeDtypeStruct((peers, 2, t...  6.68 us
    pallas_call x1, Pallas kernels, own_keys(): pl.pallas_call(own_keys_kernel, out_shape=(jax.ShapeDtypeStruct((rows, 10...  6.24 us
  transfers between devices with their start and end apart: 22, of which 4 were waited for; matrix products, arithmetic and copies ran while one was open for 2% of the time, Pallas kernels for 9%

profile of v2, /device:TPU:1, one launch (start us, length us, event | category | flops | bytes accessed | tf_op | source)
XLA Modules:
  0.0 206.2 jit_solution(7882380090752578104)
XLA Ops:
  0.6 2.2 %collective-permute-start = (bf16[128,1024]{1,0:T(8,128)(2,1)}, bf16[128,1024]{1,0:T(8,128)(2,1)S(1)}, u32[]{:S(2)}, u32[]{:S(2)}) collective-permute-start(bf16[128,1024]{1,0:T(8,128)(2,1)} %bitcast.43), channel_id=1, source_target_pairs={{0,16},{1,17},{2,18},{3,19},{4,20},{5,21},{6,22},{7,23},{8,24},{9,... | collective-permute-start | bytes 786440 | tf_op jit(solution)/shard_map/ppermute | solution.py:40
  2.8 0.1 collective-permute-start.1
  2.9 2.8 %pack_last.1 = (bf16[32,2,4352]{2,1,0:T(2,128)(2,1)}, f32[2,4096]{1,0:T(2,128)}) custom-call(s32[1]{0:T(128)} %bitcast.3.dev_ref, s32[64]{0:T(128)} %len_ref.3, bf16[1024,4096]{1,0:T(8,128)(2,1)} %bitcast.36, bf16[1024,4096]{1,0:T(8,128)(2,1)} %bitcast.37, bf16[1,128]{1,0:T(2,128)(2,1)} %ga_ref.1, bf16[1,128]{1,0:T(2,128)(2,1)} %gm_ref.1, bf16[1,128]{1,0:T(2,128)(2,1)} %gf_ref.1), custom_call_target="tpu_custom_call" | custom-call | tf_op jit(solution)/shard_map/pack_last/pallas_call | solution.py:119
  5.7 9.1 %all-to-all-start = ((bf16[32,2,4352]{2,1,0:T(2,128)(2,1)}), bf16[32,2,4352]{2,1,0:T(2,128)(2,1)S(1)}, u32[]{:S(2)}, u32[]{:S(2)}) async-start(bf16[32,2,4352]{2,1,0:T(2,128)(2,1)} %get-tuple-element.15), calls=%async_computation | async-start | bytes 1114112 | tf_op jit(solution)/shard_map/all_to_all | solution.py:64
  14.8 0.2 copy.19
  15.0 0.1 copy.20
  15.2 0.1 fusion.value_ref
  15.3 0.1 multiply_convert_fusion.2
  15.4 0.1 multiply_convert_fusion.1
  15.6 2.8 %collective-permute-start.6 = (bf16[256,512]{1,0:T(8,128)(2,1)S(1)}, bf16[256,512]{1,0:T(8,128)(2,1)S(1)}, u32[]{:S(2)}, u32[]{:S(2)}) collective-permute-start(bf16[256,512]{1,0:T(8,128)(2,1)S(1)} %get-tuple-element.22), channel_id=1, source_target_pairs={{0,2},{1,3},{2,0},{3,1},{4,6},{5,7},{6,4},{7,5},{8,10},{9,11},{10,... | collective-permute-start | bytes 786440 | tf_op jit(solution)/shard_map/ppermute | solution.py:40
  18.4 0.3 collective-permute-start.7
  18.7 2.4 %collective-permute-start.5 = (bf16[256,512]{1,0:T(8,128)(2,1)S(1)}, bf16[256,512]{1,0:T(8,128)(2,1)S(1)}, u32[]{:S(2)}, u32[]{:S(2)}) collective-permute-start(bf16[256,512]{1,0:T(8,128)(2,1)S(1)} %get-tuple-element.22), channel_id=1, source_target_pairs={{0,3},{1,0},{2,1},{3,2},{4,7},{5,4},{6,5},{7,6},{8,11},{9,8},{10,9... | collective-permute-start | bytes 786440 | tf_op jit(solution)/shard_map/ppermute | solution.py:40
  21.1 1.3 collective-permute-start.4
  22.4 2.4 %collective-permute-start.3 = (bf16[256,512]{1,0:T(8,128)(2,1)S(1)}, bf16[256,512]{1,0:T(8,128)(2,1)S(1)}, u32[]{:S(2)}, u32[]{:S(2)}) collective-permute-start(bf16[256,512]{1,0:T(8,128)(2,1)S(1)} %get-tuple-element.23), channel_id=1, source_target_pairs={{0,8},{1,9},{2,10},{3,11},{4,12},{5,13},{6,14},{7,15},{8,0},{9,1},... | collective-permute-start | bytes 786440 | tf_op jit(solution)/shard_map/ppermute | solution.py:40
  24.8 5.5 %collective-permute-done.6 = bf16[256,512]{1,0:T(8,128)(2,1)S(1)} collective-permute-done((bf16[256,512]{1,0:T(8,128)(2,1)S(1)}, bf16[256,512]{1,0:T(8,128)(2,1)S(1)}, u32[]{:S(2)}, u32[]{:S(2)}) %collective-permute-start.6) | collective-permute-done | bytes 262176 | tf_op jit(solution)/shard_map/ppermute | solution.py:40
  30.3 2.8 %collective-permute-start.2 = (bf16[256,512]{1,0:T(8,128)(2,1)S(1)}, bf16[256,512]{1,0:T(8,128)(2,1)}, u32[]{:S(2)}, u32[]{:S(2)}) collective-permute-start(bf16[256,512]{1,0:T(8,128)(2,1)S(1)} %get-tuple-element.23), channel_id=1, source_target_pairs={{0,12},{1,13},{2,14},{3,15},{4,0},{5,1},{6,2},{7,3},{8,4},{9,5},{1... | collective-permute-start | bytes 786440 | tf_op jit(solution)/shard_map/ppermute | solution.py:40
  33.0 3.7 %collective-permute-done.7 = bf16[256,512]{1,0:T(8,128)(2,1)S(1)} collective-permute-done((bf16[256,512]{1,0:T(8,128)(2,1)S(1)}, bf16[256,512]{1,0:T(8,128)(2,1)S(1)}, u32[]{:S(2)}, u32[]{:S(2)}) %collective-permute-start.7) | collective-permute-done | bytes 262176 | tf_op jit(solution)/shard_map/ppermute | solution.py:40
  36.7 1.9 collective-permute-start.13
  38.7 0.1 collective-permute-start.14
  38.8 0.2 fusion.11
  39.0 0.1 pad_maximum_fusion.7
  39.2 0.5 collective-permute-start.9
  39.6 1.2 copy-done.10
  40.9 0.8 parcel.1
  41.7 1.0 copy-done.7
  42.7 0.6 copy-done.21
  43.3 5.6 %all-to-all-start.1 = ((bf16[32,144,128]{2,1,0:T(8,128)(2,1)}), bf16[32,144,128]{2,1,0:T(8,128)(2,1)S(1)}, u32[]{:S(2)}, u32[]{:S(2)}) async-start(bf16[32,144,128]{2,1,0:T(8,128)(2,1)} %copy-done.7), calls=%async_computation.1 | async-start | bytes 2359296 | tf_op jit(solution)/shard_map/all_to_all | solution.py:64
  49.0 1.0 pad_maximum_fusion.a_low
  50.0 1.3 collective-permute-start.10
  51.3 1.2 collective-permute-start.15
  52.5 1.5 collective-permute-start.12
  54.0 1.2 collective-permute-start.11
  55.1 1.5 collective-permute-start.8
  56.6 19.6 %collective-permute-done.10.a3l = bf16[2,256,512]{2,1,0:T(8,128)(2,1)} collective-permute-done((bf16[2,256,512]{2,1,0:T(8,128)(2,1)S(1)}, bf16[2,256,512]{2,1,0:T(8,128)(2,1)}, u32[]{:S(2)}, u32[]{:S(2)}) %collective-permute-start.10) | collective-permute-done | bytes 524320 | tf_op jit(solution)/shard_map/ppermute | solution.py:40
  76.2 2.7 %collective-permute-start.19 = (bf16[2,256,512]{2,1,0:T(8,128)(2,1)}, bf16[2,256,512]{2,1,0:T(8,128)(2,1)}, u32[]{:S(2)}, u32[]{:S(2)}) collective-permute-start(bf16[2,256,512]{2,1,0:T(8,128)(2,1)} %collective-permute-done.13.b1h), channel_id=1, source_target_pairs={{0,12},{1,13},{2,14},{3,15},{4,0},{5,1},{6,2},{7,3},{8,4},{9,5},{1... | collective-permute-start | bytes 1572872 | tf_op jit(solution)/shard_map/ppermute | solution.py:40
  78.9 0.8 copy-done.11
  79.7 0.8 copy-done.13
  80.5 0.2 collective-permute-start.17
  80.8 6.7 %collective-permute-done.11.a3h = bf16[2,256,512]{2,1,0:T(8,128)(2,1)S(1)} collective-permute-done((bf16[2,256,512]{2,1,0:T(8,128)(2,1)S(1)}, bf16[2,256,512]{2,1,0:T(8,128)(2,1)S(1)}, u32[]{:S(2)}, u32[]{:S(2)}) %collective-permute-start.11) | collective-permute-done | bytes 524320 | tf_op jit(solution)/shard_map/ppermute | solution.py:40
  87.5 0.8 copy-done.15
  88.3 0.1 pad_add_fusion.dev_ref
  88.3 1.6 fusion.4
  89.9 0.9 pad_maximum_fusion.5
  90.8 6.2 %own_keys.1 = (f32[1024,1024]{1,0:T(8,128)S(1)}, f32[1024,128]{1,0:T(8,128)S(1)}, bf16[1024,4096]{1,0:T(8,128)(2,1)S(1)}) custom-call(s32[4]{0:T(128)S(1)} %pad_add_fusion.dev_ref, bf16[1024,4096]{1,0:T(8,128)(2,1)} %bitcast.38, bf16[2,256,512]{2,1,0:T(8,128)(2,1)S(1)} %pad_maximum_fusion.a_low, bf16[2,256,512]{2,1,0:T(8,128)(2,1)S(1)} %pad_maximum_fusion.1.a_high, ...), custom_call_target="tpu_custom_call" | custom-call | tf_op jit(solution)/shard_map/own_keys/pallas_call | solution.py:236
  97.1 0.8 copy-done.17
  97.9 9.1 %near_keys.1.acc_ref = f32[1024,1024]{1,0:T(8,128)S(1)} custom-call(s32[4]{0:T(128)S(1)} %pad_add_fusion.dev_ref, bf16[1024,4096]{1,0:T(8,128)(2,1)S(1)} %get-tuple-element.12.x_ref, f32[1024,1024]{1,0:T(8,128)S(1)} %get-tuple-element.13.acc_ref, bf16[2,256,512]{2,1,0:T(8,128)(2,1)} %collective-permute-done.8.a1l, ...), custom_call_target="tpu_custom_call", output_to_operand_aliasing={{}: (2, {})} | custom-call | tf_op jit(solution)/shard_map/near_keys/pallas_call | solution.py:252
  107.0 2.1 copy-done.2
  109.2 3.4 %copy-done.1 = bf16[1024,4096]{1,0:T(8,128)(2,1)S(1)} copy-done((bf16[1024,4096]{1,0:T(8,128)(2,1)S(1)}, bf16[1024,4096]{1,0:T(8,128)(2,1)}, u32[]{:S(2)}) %copy-start.1) | copy-done | bytes 8388632
  112.5 2.2 %copy-done.3 = f32[1024,1024]{1,0:T(8,128)S(1)} copy-done((f32[1024,1024]{1,0:T(8,128)S(1)}, f32[1024,1024]{1,0:T(8,128)}, u32[]{:S(2)}) %copy-start.3) | copy-done | bytes 4194328
  114.7 0.7 copy-done.24
  115.4 6.7 %attend.1 = bf16[32,2,4096]{2,1,0:T(2,128)(2,1)S(1)} custom-call(s32[4]{0:T(128)S(1)} %copy-done.24, s32[64]{0:T(128)S(1)} %copy-done.26, bf16[1024,4096]{1,0:T(8,128)(2,1)S(1)} %copy-done.1, f32[1024,1024]{1,0:T(8,128)S(1)} %copy-done.3, f32[1024,128]{1,0:T(8,128)S(1)} %copy-done.18, bf16[2,256,512]{2,1,0:T(8,128)(2,1)} %collective-permute-done.16.a_low, ...), custom_call_target="tpu_custom_call" | custom-call | tf_op jit(solution)/shard_map/attend/pallas_call | solution.py:318
  122.1 17.2 %all_to_all.35.x_ref = bf16[32,2,4096]{2,1,0:T(2,128)(2,1)S(1)} all-to-all(bf16[32,2,4096]{2,1,0:T(2,128)(2,1)S(1)} %attend.1), channel_id=1, replica_groups=mesh['judge'=4,'fsdp'=32] {'fsdp'}, dimensions={0} | all-to-all | bytes 1048576 | tf_op jit(solution)/shard_map/all_to_all | solution.py:64
  139.3 0.7 mix.1
  140.0 14.0 %all_to_all.36.parts_ref = bf16[32,2,4096]{2,1,0:T(2,128)(2,1)S(1)} all-to-all(bf16[32,2,4096]{2,1,0:T(2,128)(2,1)S(1)} %mix.1), channel_id=1, replica_groups=mesh['judge'=4,'fsdp'=32] {'fsdp'}, dimensions={0} | all-to-all | bytes 1048576 | tf_op jit(solution)/shard_map/all_to_all | solution.py:64
  153.9 0.3 middle.1
  154.2 12.7 %all_to_all.37.x_ref = bf16[32,2,4096]{2,1,0:T(2,128)(2,1)S(1)} all-to-all(bf16[32,2,4096]{2,1,0:T(2,128)(2,1)S(1)} %get-tuple-element.19), channel_id=1, replica_groups=mesh['judge'=4,'fsdp'=32] {'fsdp'}, dimensions={0} | all-to-all | bytes 1048576 | tf_op jit(solution)/shard_map/all_to_all | solution.py:64
  166.9 2.9 %mlp.1 = bf16[32,2,4096]{2,1,0:T(2,128)(2,1)S(1)} custom-call(bf16[32,2,4096]{2,1,0:T(2,128)(2,1)S(1)} %all_to_all.37.x_ref, bf16[448,4096]{1,0:T(8,128)(2,1)S(1)} %bitcast.31, bf16[448,4096]{1,0:T(8,128)(2,1)S(1)} %bitcast.32, bf16[448,4096]{1,0:T(8,128)(2,1)S(1)} %bitcast.33), custom_call_target="tpu_custom_call" | custom-call | tf_op jit(solution)/shard_map/mlp/pallas_call | solution.py:392
  169.8 13.1 %all_to_all.38.parts_ref = bf16[32,2,4096]{2,1,0:T(2,128)(2,1)S(1)} all-to-all(bf16[32,2,4096]{2,1,0:T(2,128)(2,1)S(1)} %mlp.1), channel_id=1, replica_groups=mesh['judge'=4,'fsdp'=32] {'fsdp'}, dimensions={0} | all-to-all | bytes 1048576 | tf_op jit(solution)/shard_map/all_to_all | solution.py:64
  182.9 0.3 finish.1
  183.2 21.5 %all_to_all.39 = f32[128,1,384]{2,1,0:T(1,128)S(1)} all-to-all(f32[128,1,384]{2,1,0:T(1,128)S(1)} %finish.1), channel_id=1, replica_groups=mesh['judge'=4,'fsdp'=32] {'judge','fsdp'}, dimensions={0} | all-to-all | bytes 393216 | tf_op jit(solution)/shard_map/all_to_all | solution.py:64
  204.9 0.1 reshape.57
  205.0 0.2 fusion.5
  205.2 0.2 fusion.6
  205.4 0.9 fusion.7
  (91 shorter events, 0.4 us)
Async XLA Ops:
  0.6 14.8 %collective-permute-start = (bf16[128,1024]{1,0:T(8,128)(2,1)}, bf16[128,1024]{1,0:T(8,128)(2,1)S(1)}, u32[]{:S(2)}, u32[]{:S(2)}) collective-permute-start(bf16[128,1024]{1,0:T(8,128)(2,1)} %bitcast.43), channel_id=1, source_target_pairs={{0,16},{1,17},{2,18},{3,19},{4,20},{5,21},{6,22},{7,23},{8,24},{9,... | collective-permute-start | bytes 786440 | tf_op jit(solution)/shard_map/ppermute | solution.py:40
  2.8 12.6 %collective-permute-start.1 = (bf16[128]{0:T(256)(128)(2,1)}, bf16[128]{0:T(256)(128)(2,1)S(1)}, u32[]{:S(2)}, u32[]{:S(2)}) collective-permute-start(bf16[128]{0:T(256)(128)(2,1)} %bitcast.49), channel_id=1, source_target_pairs={{0,16},{1,17},{2,18},{3,19},{4,20},{5,21},{6,22},{7,23},{8,24},{9,... | collective-permute-start | bytes 776 | tf_op jit(solution)/shard_map/ppermute | solution.py:40
  2.9 11.9 %copy-start.31 = (bf16[1,128]{1,0:T(2,128)(2,1)S(1)}, bf16[1,128]{1,0:T(2,128)(2,1)}, u32[]{:S(2)}) copy-start(bf16[1,128]{1,0:T(2,128)(2,1)} %ga_ref.1) | copy-start | bytes 772
  2.9 11.9 %copy-start.28 = (bf16[1,128,1024]{2,1,0:T(8,128)(2,1)S(1)}, bf16[1,128,1024]{2,1,0:T(8,128)(2,1)}, u32[]{:S(2)}) copy-start(bf16[1,128,1024]{2,1,0:T(8,128)(2,1)} %param.20) | copy-start | bytes 786436
  2.9 12.4 %copy-start.27 = (bf16[1,128,1024]{2,1,0:T(8,128)(2,1)S(1)}, bf16[1,128,1024]{2,1,0:T(8,128)(2,1)}, u32[]{:S(2)}) copy-start(bf16[1,128,1024]{2,1,0:T(8,128)(2,1)} %param.19) | copy-start | bytes 786436
  5.7 15.4 %copy-start.25 = (s32[64]{0:T(128)S(1)}, s32[64]{0:T(128)}, u32[]{:S(2)}) copy-start(s32[64]{0:T(128)} %len_ref.3) | copy-start | bytes 772
  5.7 34.0 %all-to-all-start = ((bf16[32,2,4352]{2,1,0:T(2,128)(2,1)}), bf16[32,2,4352]{2,1,0:T(2,128)(2,1)S(1)}, u32[]{:S(2)}, u32[]{:S(2)}) async-start(bf16[32,2,4352]{2,1,0:T(2,128)(2,1)} %get-tuple-element.15), calls=%async_computation | async-start | bytes 1114112 | tf_op jit(solution)/shard_map/all_to_all | solution.py:64
  15.6 14.7 %collective-permute-start.6 = (bf16[256,512]{1,0:T(8,128)(2,1)S(1)}, bf16[256,512]{1,0:T(8,128)(2,1)S(1)}, u32[]{:S(2)}, u32[]{:S(2)}) collective-permute-start(bf16[256,512]{1,0:T(8,128)(2,1)S(1)} %get-tuple-element.22), channel_id=1, source_target_pairs={{0,2},{1,3},{2,0},{3,1},{4,6},{5,7},{6,4},{7,5},{8,10},{9,11},{10,... | collective-permute-start | bytes 786440 | tf_op jit(solution)/shard_map/ppermute | solution.py:40
  18.4 18.3 %collective-permute-start.7 = (bf16[256,512]{1,0:T(8,128)(2,1)S(1)}, bf16[256,512]{1,0:T(8,128)(2,1)S(1)}, u32[]{:S(2)}, u32[]{:S(2)}) collective-permute-start(bf16[256,512]{1,0:T(8,128)(2,1)S(1)} %get-tuple-element.22), channel_id=1, source_target_pairs={{0,1},{1,2},{2,3},{3,0},{4,5},{5,6},{6,7},{7,4},{8,9},{9,10},{10,1... | collective-permute-start | bytes 786440 | tf_op jit(solution)/shard_map/ppermute | solution.py:40
  18.7 20.0 %collective-permute-start.5 = (bf16[256,512]{1,0:T(8,128)(2,1)S(1)}, bf16[256,512]{1,0:T(8,128)(2,1)S(1)}, u32[]{:S(2)}, u32[]{:S(2)}) collective-permute-start(bf16[256,512]{1,0:T(8,128)(2,1)S(1)} %get-tuple-element.22), channel_id=1, source_target_pairs={{0,3},{1,0},{2,1},{3,2},{4,7},{5,4},{6,5},{7,6},{8,11},{9,8},{10,9... | collective-permute-start | bytes 786440 | tf_op jit(solution)/shard_map/ppermute | solution.py:40
  21.1 18.5 %copy-start.30 = (f32[64]{0:T(128)}, f32[64]{0:T(128)S(1)}, u32[]{:S(2)}) copy-start(f32[64]{0:T(128)S(1)} %multiply_exponential_fusion) | copy-start | bytes 772
  21.1 18.0 %collective-permute-start.4 = (bf16[256,512]{1,0:T(8,128)(2,1)S(1)}, bf16[256,512]{1,0:T(8,128)(2,1)S(1)}, u32[]{:S(2)}, u32[]{:S(2)}) collective-permute-start(bf16[256,512]{1,0:T(8,128)(2,1)S(1)} %get-tuple-element.23), channel_id=1, source_target_pairs={{0,4},{1,5},{2,6},{3,7},{4,8},{5,9},{6,10},{7,11},{8,12},{9,13},{1... | collective-permute-start | bytes 786440 | tf_op jit(solution)/shard_map/ppermute | solution.py:40
  22.4 16.7 %collective-permute-start.3 = (bf16[256,512]{1,0:T(8,128)(2,1)S(1)}, bf16[256,512]{1,0:T(8,128)(2,1)S(1)}, u32[]{:S(2)}, u32[]{:S(2)}) collective-permute-start(bf16[256,512]{1,0:T(8,128)(2,1)S(1)} %get-tuple-element.23), channel_id=1, source_target_pairs={{0,8},{1,9},{2,10},{3,11},{4,12},{5,13},{6,14},{7,15},{8,0},{9,1},... | collective-permute-start | bytes 786440 | tf_op jit(solution)/shard_map/ppermute | solution.py:40
  30.3 18.7 %collective-permute-start.2 = (bf16[256,512]{1,0:T(8,128)(2,1)S(1)}, bf16[256,512]{1,0:T(8,128)(2,1)}, u32[]{:S(2)}, u32[]{:S(2)}) collective-permute-start(bf16[256,512]{1,0:T(8,128)(2,1)S(1)} %get-tuple-element.23), channel_id=1, source_target_pairs={{0,12},{1,13},{2,14},{3,15},{4,0},{5,1},{6,2},{7,3},{8,4},{9,5},{1... | collective-permute-start | bytes 786440 | tf_op jit(solution)/shard_map/ppermute | solution.py:40
  36.7 15.7 %collective-permute-start.13 = (bf16[2,256,512]{2,1,0:T(8,128)(2,1)S(1)}, bf16[2,256,512]{2,1,0:T(8,128)(2,1)}, u32[]{:S(2)}, u32[]{:S(2)}) collective-permute-start(bf16[2,256,512]{2,1,0:T(8,128)(2,1)S(1)} %pad_maximum_fusion.3.b_high), channel_id=1, source_target_pairs={{0,12},{1,13},{2,14},{3,15},{4,0},{5,1},{6,2},{7,3},{8,4},{9,5},{1... | collective-permute-start | bytes 1572872 | tf_op jit(solution)/shard_map/ppermute | solution.py:40
  38.7 15.2 %collective-permute-start.14 = (bf16[2,256,512]{2,1,0:T(8,128)(2,1)S(1)}, bf16[2,256,512]{2,1,0:T(8,128)(2,1)}, u32[]{:S(2)}, u32[]{:S(2)}) collective-permute-start(bf16[2,256,512]{2,1,0:T(8,128)(2,1)S(1)} %pad_maximum_fusion.2.b_low), channel_id=1, source_target_pairs={{0,4},{1,5},{2,6},{3,7},{4,8},{5,9},{6,10},{7,11},{8,12},{9,13},{1... | collective-permute-start | bytes 1572872 | tf_op jit(solution)/shard_map/ppermute | solution.py:40
  39.2 16.0 %collective-permute-start.9 = (bf16[2,256,512]{2,1,0:T(8,128)(2,1)S(1)}, bf16[2,256,512]{2,1,0:T(8,128)(2,1)}, u32[]{:S(2)}, u32[]{:S(2)}) collective-permute-start(bf16[2,256,512]{2,1,0:T(8,128)(2,1)S(1)} %pad_maximum_fusion.1.a_high), channel_id=1, source_target_pairs={{0,3},{1,0},{2,1},{3,2},{4,7},{5,4},{6,5},{7,6},{8,11},{9,8},{10,9... | collective-permute-start | bytes 1572872 | tf_op jit(solution)/shard_map/ppermute | solution.py:40
  39.6 1.2 copy-start.10
  41.7 1.0 copy-start.7
  42.7 0.6 copy-start.21
  43.3 65.8 %all-to-all-start.1 = ((bf16[32,144,128]{2,1,0:T(8,128)(2,1)}), bf16[32,144,128]{2,1,0:T(8,128)(2,1)S(1)}, u32[]{:S(2)}, u32[]{:S(2)}) async-start(bf16[32,144,128]{2,1,0:T(8,128)(2,1)} %copy-done.7), calls=%async_computation.1 | async-start | bytes 2359296 | tf_op jit(solution)/shard_map/all_to_all | solution.py:64
  50.0 26.2 %collective-permute-start.10 = (bf16[2,256,512]{2,1,0:T(8,128)(2,1)S(1)}, bf16[2,256,512]{2,1,0:T(8,128)(2,1)}, u32[]{:S(2)}, u32[]{:S(2)}) collective-permute-start(bf16[2,256,512]{2,1,0:T(8,128)(2,1)S(1)} %pad_maximum_fusion.a_low), channel_id=1, source_target_pairs={{0,1},{1,2},{2,3},{3,0},{4,5},{5,6},{6,7},{7,4},{8,9},{9,10},{10,1... | collective-permute-start | bytes 1572872 | tf_op jit(solution)/shard_map/ppermute | solution.py:40
  51.3 27.7 %collective-permute-start.15 = (bf16[2,256,512]{2,1,0:T(8,128)(2,1)S(1)}, bf16[2,256,512]{2,1,0:T(8,128)(2,1)S(1)}, u32[]{:S(2)}, u32[]{:S(2)}) collective-permute-start(bf16[2,256,512]{2,1,0:T(8,128)(2,1)S(1)} %pad_maximum_fusion.3.b_high), channel_id=1, source_target_pairs={{0,4},{1,5},{2,6},{3,7},{4,8},{5,9},{6,10},{7,11},{8,12},{9,13},{1... | collective-permute-start | bytes 1572872 | tf_op jit(solution)/shard_map/ppermute | solution.py:40
  52.5 27.3 %collective-permute-start.12 = (bf16[2,256,512]{2,1,0:T(8,128)(2,1)S(1)}, bf16[2,256,512]{2,1,0:T(8,128)(2,1)S(1)}, u32[]{:S(2)}, u32[]{:S(2)}) collective-permute-start(bf16[2,256,512]{2,1,0:T(8,128)(2,1)S(1)} %pad_maximum_fusion.2.b_low), channel_id=1, source_target_pairs={{0,12},{1,13},{2,14},{3,15},{4,0},{5,1},{6,2},{7,3},{8,4},{9,5},{1... | collective-permute-start | bytes 1572872 | tf_op jit(solution)/shard_map/ppermute | solution.py:40
  54.0 33.5 %collective-permute-start.11 = (bf16[2,256,512]{2,1,0:T(8,128)(2,1)S(1)}, bf16[2,256,512]{2,1,0:T(8,128)(2,1)S(1)}, u32[]{:S(2)}, u32[]{:S(2)}) collective-permute-start(bf16[2,256,512]{2,1,0:T(8,128)(2,1)S(1)} %pad_maximum_fusion.1.a_high), channel_id=1, source_target_pairs={{0,1},{1,2},{2,3},{3,0},{4,5},{5,6},{6,7},{7,4},{8,9},{9,10},{10,1... | collective-permute-start | bytes 1572872 | tf_op jit(solution)/shard_map/ppermute | solution.py:40
  55.1 42.7 %collective-permute-start.8 = (bf16[2,256,512]{2,1,0:T(8,128)(2,1)S(1)}, bf16[2,256,512]{2,1,0:T(8,128)(2,1)}, u32[]{:S(2)}, u32[]{:S(2)}) collective-permute-start(bf16[2,256,512]{2,1,0:T(8,128)(2,1)S(1)} %pad_maximum_fusion.a_low), channel_id=1, source_target_pairs={{0,3},{1,0},{2,1},{3,2},{4,7},{5,4},{6,5},{7,6},{8,11},{9,8},{10,9... | collective-permute-start | bytes 1572872 | tf_op jit(solution)/shard_map/ppermute | solution.py:40
  76.2 32.9 %collective-permute-start.19 = (bf16[2,256,512]{2,1,0:T(8,128)(2,1)}, bf16[2,256,512]{2,1,0:T(8,128)(2,1)}, u32[]{:S(2)}, u32[]{:S(2)}) collective-permute-start(bf16[2,256,512]{2,1,0:T(8,128)(2,1)} %collective-permute-done.13.b1h), channel_id=1, source_target_pairs={{0,12},{1,13},{2,14},{3,15},{4,0},{5,1},{6,2},{7,3},{8,4},{9,5},{1... | collective-permute-start | bytes 1572872 | tf_op jit(solution)/shard_map/ppermute | solution.py:40
  78.9 0.8 copy-start.11
  79.7 29.4 %collective-permute-start.18 = (bf16[2,256,512]{2,1,0:T(8,128)(2,1)}, bf16[2,256,512]{2,1,0:T(8,128)(2,1)}, u32[]{:S(2)}, u32[]{:S(2)}) collective-permute-start(bf16[2,256,512]{2,1,0:T(8,128)(2,1)} %collective-permute-done.14.b3l), channel_id=1, source_target_pairs={{0,4},{1,5},{2,6},{3,7},{4,8},{5,9},{6,10},{7,11},{8,12},{9,13},{1... | collective-permute-start | bytes 1572872 | tf_op jit(solution)/shard_map/ppermute | solution.py:40
  79.7 0.8 copy-start.13
  80.5 28.6 %collective-permute-start.17 = (bf16[2,256,512]{2,1,0:T(8,128)(2,1)}, bf16[2,256,512]{2,1,0:T(8,128)(2,1)}, u32[]{:S(2)}, u32[]{:S(2)}) collective-permute-start(bf16[2,256,512]{2,1,0:T(8,128)(2,1)} %collective-permute-done.9.a1h), channel_id=1, source_target_pairs={{0,3},{1,0},{2,1},{3,2},{4,7},{5,4},{6,5},{7,6},{8,11},{9,8},{10,9... | collective-permute-start | bytes 1572872 | tf_op jit(solution)/shard_map/ppermute | solution.py:40
  87.5 0.8 copy-start.15
  88.3 20.8 %collective-permute-start.16 = (bf16[2,256,512]{2,1,0:T(8,128)(2,1)}, bf16[2,256,512]{2,1,0:T(8,128)(2,1)}, u32[]{:S(2)}, u32[]{:S(2)}) collective-permute-start(bf16[2,256,512]{2,1,0:T(8,128)(2,1)} %collective-permute-done.10.a3l), channel_id=1, source_target_pairs={{0,1},{1,2},{2,3},{3,0},{4,5},{5,6},{6,7},{7,4},{8,9},{9,10},{10,1... | collective-permute-start | bytes 1572872 | tf_op jit(solution)/shard_map/ppermute | solution.py:40
  88.3 9.5 %copy-start.23 = (s32[4]{0:T(128)}, s32[4]{0:T(128)S(1)}, u32[]{:S(2)}) copy-start(s32[4]{0:T(128)S(1)} %pad_add_fusion.dev_ref) | copy-start | bytes 52
  90.8 7.1 %copy-start.12 = (bf16[2,256,512]{2,1,0:T(8,128)(2,1)S(1)}, bf16[2,256,512]{2,1,0:T(8,128)(2,1)}, u32[]{:S(2)}) copy-start(bf16[2,256,512]{2,1,0:T(8,128)(2,1)} %copy-done.11) | copy-start | bytes 1572868
  90.8 7.1 %copy-start.14 = (bf16[2,256,512]{2,1,0:T(8,128)(2,1)S(1)}, bf16[2,256,512]{2,1,0:T(8,128)(2,1)}, u32[]{:S(2)}) copy-start(bf16[2,256,512]{2,1,0:T(8,128)(2,1)} %copy-done.13) | copy-start | bytes 1572868
  90.8 7.1 %copy-start.16 = (bf16[2,256,512]{2,1,0:T(8,128)(2,1)S(1)}, bf16[2,256,512]{2,1,0:T(8,128)(2,1)}, u32[]{:S(2)}) copy-start(bf16[2,256,512]{2,1,0:T(8,128)(2,1)} %copy-done.15) | copy-start | bytes 1572868
  97.1 0.8 copy-start.17
  97.9 9.2 %copy-start = (bf16[1024,4096]{1,0:T(8,128)(2,1)}, bf16[1024,4096]{1,0:T(8,128)(2,1)S(1)}, u32[]{:S(2)}) copy-start(bf16[1024,4096]{1,0:T(8,128)(2,1)S(1)} %get-tuple-element.12.x_ref) | copy-start | bytes 25165828
  97.9 11.2 %copy-start.8 = (f32[512,128]{1,0:T(8,128)S(1)}, f32[512,128]{1,0:T(8,128)}, u32[]{:S(2)}) copy-start(f32[512,128]{1,0:T(8,128)} %get-tuple-element.33.sin_ref) | copy-start | bytes 786436
  97.9 11.2 %copy-start.18 = (f32[1024,128]{1,0:T(8,128)S(1)}, f32[1024,128]{1,0:T(8,128)}, u32[]{:S(2)}) copy-start(f32[1024,128]{1,0:T(8,128)} %copy-done.17) | copy-start | bytes 1572868
  97.9 11.2 %copy-start.26 = (s32[64]{0:T(128)S(1)}, s32[64]{0:T(128)}, u32[]{:S(2)}) copy-start(s32[64]{0:T(128)} %len_ref.3) | copy-start | bytes 772
  107.0 2.1 %copy-start.2 = (f32[1024,1024]{1,0:T(8,128)}, f32[1024,1024]{1,0:T(8,128)S(1)}, u32[]{:S(2)}) copy-start(f32[1024,1024]{1,0:T(8,128)S(1)} %near_keys.1.acc_ref) | copy-start | bytes 12582916
  109.2 3.4 %copy-start.1 = (bf16[1024,4096]{1,0:T(8,128)(2,1)S(1)}, bf16[1024,4096]{1,0:T(8,128)(2,1)}, u32[]{:S(2)}) copy-start(bf16[1024,4096]{1,0:T(8,128)(2,1)} %copy-done) | copy-start | bytes 25165828
  112.5 2.2 %copy-start.3 = (f32[1024,1024]{1,0:T(8,128)S(1)}, f32[1024,1024]{1,0:T(8,128)}, u32[]{:S(2)}) copy-start(f32[1024,1024]{1,0:T(8,128)} %copy-done.2) | copy-start | bytes 12582916
  114.7 0.7 copy-start.24
  115.4 23.9 %copy-start.9 = (bf16[1,128,4096]{2,1,0:T(8,128)(2,1)S(1)}, bf16[1,128,4096]{2,1,0:T(8,128)(2,1)}, u32[]{:S(2)}) copy-start(bf16[1,128,4096]{2,1,0:T(8,128)(2,1)} %param.21) | copy-start | bytes 3145732
  115.4 51.5 %copy-start.5 = (bf16[1,4096,448]{1,2,0:T(8,128)(2,1)S(1)}, bf16[1,4096,448]{1,2,0:T(8,128)(2,1)}, u32[]{:S(2)}) copy-start(bf16[1,4096,448]{1,2,0:T(8,128)(2,1)} %param.24) | copy-start | bytes 11010052
  115.4 51.5 %copy-start.6 = (bf16[1,448,4096]{2,1,0:T(8,128)(2,1)S(1)}, bf16[1,448,4096]{2,1,0:T(8,128)(2,1)}, u32[]{:S(2)}) copy-start(bf16[1,448,4096]{2,1,0:T(8,128)(2,1)} %param.25) | copy-start | bytes 11010052
  122.1 31.9 %copy-start.19 = (f32[2,4096]{1,0:T(2,128)S(1)}, f32[2,4096]{1,0:T(2,128)}, u32[]{:S(2)}) copy-start(f32[2,4096]{1,0:T(2,128)} %get-tuple-element.17.own_ref) | copy-start | bytes 98308
  122.1 31.8 %copy-start.22 = (f32[1,4096]{1,0:T(1,128)S(1)}, f32[1,4096]{1,0:T(1,128)}, u32[]{:S(2)}) copy-start(f32[1,4096]{1,0:T(1,128)} %copy-done.21) | copy-start | bytes 49156
  122.1 44.8 %copy-start.4 = (bf16[1,4096,448]{1,2,0:T(8,128)(2,1)S(1)}, bf16[1,4096,448]{1,2,0:T(8,128)(2,1)}, u32[]{:S(2)}) copy-start(bf16[1,4096,448]{1,2,0:T(8,128)(2,1)} %param.23) | copy-start | bytes 11010052
  166.9 16.0 %copy-start.20 = (f32[1,4096]{1,0:T(1,128)S(1)}, f32[1,4096]{1,0:T(1,128)}, u32[]{:S(2)}) copy-start(f32[1,4096]{1,0:T(1,128)} %head_ref.1) | copy-start | bytes 49156
  166.9 38.0 %copy-start.29 = (s32[64]{0:T(128)S(1)}, s32[64]{0:T(128)}, u32[]{:S(2)}) copy-start(s32[64]{0:T(128)} %param.16) | copy-start | bytes 772
  205.4 0.9 copy-start.32

commit v3 on v2

--- a/solution.py
+++ b/solution.py
@@ -1,3 +1,4 @@
+import functools
 import math
 
 import jax
@@ -215,17 +216,21 @@
         sum_ref[rows, :] = jnp.broadcast_to(jnp.sum(x * x, axis=1, keepdims=True), (ROWS, 128))
 
 
-def near_keys_kernel(dev_ref, x_ref, acc_ref, a1l, a1h, a3l, a3h, b1l, b1h, b3l, b3h, out_ref):
+def more_keys_kernel(parts, dev_ref, x_ref, acc_ref, *refs):
+    out_ref = refs[-1]
+
     def step(i, carry):
         rows = pl.ds(pl.multiple_of(i * ROWS, ROWS), ROWS)
-        first = acc_ref[rows, :512]
-        first += times(columns(x_ref, rows, dev_ref, z_group(1)), a1l, a1h)
-        first += times(columns(x_ref, rows, dev_ref, z_group(3)), a3l, a3h)
-        out_ref[rows, :512] = first
-        second = acc_ref[rows, 512:]
-        second += times(columns(x_ref, rows, dev_ref, x_group(1)), b1l, b1h)
-        second += times(columns(x_ref, rows, dev_ref, x_group(3)), b3l, b3h)
-        out_ref[rows, 512:] = second
+        for at, group in ((0, z_group), (512, x_group)):
+            cols = slice(at, at + 512)
+            total = acc_ref[rows, cols]
+            for (side, off, half), w_ref in zip(parts, refs):
+                if side == at:
+                    lhs = columns(x_ref, rows, dev_ref, group(off)[2 * half : 2 * half + 2])
+                    total += jnp.dot(
+                        lhs, w_ref[...].reshape(512, -1), preferred_element_type=jnp.float32
+                    )
+            out_ref[rows, cols] = total
         return carry
 
     lax.fori_loop(0, x_ref.shape[0] // ROWS, step, 0)
@@ -248,16 +253,15 @@
     )(dev, pltpu.with_memory_space_constraint(tokens, pltpu.HBM), *parts)
 
 
-def near_keys(dev, tokens, acc, parts):
-    return pl.pallas_call(
-        near_keys_kernel,
+def more_keys(dev, tokens, acc, parts, arrays):
+    return pl.pallas_call(
+        functools.partial(more_keys_kernel, parts),
         out_shape=jax.ShapeDtypeStruct(acc.shape, jnp.float32),
-        in_specs=[SMEM] + [VMEM] * 10,
+        in_specs=[SMEM] + [VMEM] * (2 + len(arrays)),
         out_specs=VMEM,
         input_output_aliases={2: 0},
         compiler_params=pltpu.CompilerParams(vmem_limit_bytes=NEAR_LIMIT),
-        name="near_keys",
-    )(dev, tokens, acc, *parts)
+    )(dev, tokens, acc, *arrays)
 
 
 def attend_kernel(
@@ -268,8 +272,6 @@
     sum_ref,
     a_low,
     a_high,
-    b_low,
-    b_high,
     q_ref,
     cos_ref,
     sin_ref,
@@ -286,7 +288,7 @@
         rows = pl.ds(c * LEN, LEN)
         halves = (
             acc_ref[rows, :512] + times(columns(x_ref, rows, dev_ref, z_group(2)), a_low, a_high),
-            acc_ref[rows, 512:] + times(columns(x_ref, rows, dev_ref, x_group(2)), b_low, b_high),
+            acc_ref[rows, 512:],
         )
         parts = []
         for k in range(KV_HEADS):
@@ -319,7 +321,7 @@
         attend_kernel,
         out_shape=jax.ShapeDtypeStruct((peers, 2, tokens.shape[1]), jnp.bfloat16),
         grid=(1,),
-        in_specs=[SMEM, SMEM] + [VMEM] * 7 + [queries, VMEM, VMEM],
+        in_specs=[SMEM, SMEM] + [VMEM] * 5 + [queries, VMEM, VMEM],
         out_specs=VMEM,
         compiler_params=pltpu.CompilerParams(vmem_limit_bytes=ATTEND_LIMIT),
         name="attend",
@@ -490,14 +492,19 @@
     both = exchanged(parcel, "fsdp")
 
     acc, sums, near_tokens = own_keys(dev, tokens, (*line_x, *line_z))
-    acc = near_keys(dev, near_tokens, acc, (*near_z, *near_x))
+    (a1l, a1h, a3l, a3h), (b1l, b1h, b3l, b3h) = near_z, near_x
+    first = ((0, 1, 1), (0, 3, 0), (512, 1, 1), (512, 3, 0))
+    acc = more_keys(dev, near_tokens, acc, first, (a1h, a3l, b1h, b3l))
+    second = ((0, 1, 0), (0, 3, 1), (512, 1, 0), (512, 3, 1))
+    acc = more_keys(dev, near_tokens, acc, second, (a1l, a3h, b1l, b3h))
+    acc = more_keys(dev, near_tokens, acc, ((512, 2, 0), (512, 2, 1)), far_x)
     pooled = attend(
         dev,
         lengths,
         near_tokens,
         acc,
         sums,
-        (*far_z, *far_x),
+        far_z,
         both,
         *tables,
     )

time: 207 us -> 210 us (1.014)
  Pallas kernels: 29.7 us -> 33.3 us
    pallas_call x1 -> x3, Pallas kernels: 9.08 us -> 13.5 us  [more_keys(): pl.pallas_call(functools.partial(more_keys_kernel, parts), out_shape=jax....]
    unnamed x68 -> x64, local copies, waits for them, and re-layouts: 14.6 us -> 14.6 us
  transfers between devices with their start and end apart: 22 -> 22, of which waited for: 4 -> 4; matrix products, arithmetic and copies ran while one was open for 2% -> 2% of each run, Pallas kernels for 9% -> 11%
where the time goes in v3:
time: 210 us; the launch traced here: 209 us
  blocking collectives  78.6 us (37%)
  starting transfers between devices  41 us (20%)
  waiting for transfers between devices  35.5 us (17%)
  Pallas kernels  33.3 us (16%)
  local copies, waits for them, and re-layouts  14.8 us (7%)
  other arithmetic  4.18 us (2%)
    all_to_all x5, blocking collectives, exchanged(): return lax.all_to_all(x, axis, 0, 0, tiled=True)  78.6 us
    ppermute x20, waiting for transfers between devices, moved(): return lax.ppermute(v, 'fsdp', pairs)  35.5 us
    ppermute x20, starting transfers between devices, moved(): return lax.ppermute(v, 'fsdp', pairs)  26.2 us
    all_to_all x2, starting transfers between devices, exchanged(): return lax.all_to_all(x, axis, 0, 0, tiled=True)  14.8 us
    unnamed x64, local copies, waits for them, and re-layouts  14.6 us
    pallas_call x3, Pallas kernels, more_keys(): pl.pallas_call(functools.partial(more_keys_kernel, parts), out_shape=jax....  13.5 us
    pallas_call x1, Pallas kernels, own_keys(): pl.pallas_call(own_keys_kernel, out_shape=(jax.ShapeDtypeStruct((rows, 10...  6.19 us
    pallas_call x1, Pallas kernels, attend(): pl.pallas_call(attend_kernel, out_shape=jax.ShapeDtypeStruct((peers, 2, t...  5.91 us
  transfers between devices with their start and end apart: 22, of which 4 were waited for; matrix products, arithmetic and copies ran while one was open for 2% of the time, Pallas kernels for 11%

profile of v3, /device:TPU:1, one launch (start us, length us, event | category | flops | bytes accessed | tf_op | source)
XLA Modules:
  0.0 209.5 jit_solution(4107400073756152817)
XLA Ops:
  0.6 2.2 %collective-permute-start = (bf16[128,1024]{1,0:T(8,128)(2,1)}, bf16[128,1024]{1,0:T(8,128)(2,1)S(1)}, u32[]{:S(2)}, u32[]{:S(2)}) collective-permute-start(bf16[128,1024]{1,0:T(8,128)(2,1)} %bitcast.43), channel_id=1, source_target_pairs={{0,16},{1,17},{2,18},{3,19},{4,20},{5,21},{6,22},{7,23},{8,24},{9,... | collective-permute-start | bytes 786440 | tf_op jit(solution)/shard_map/ppermute | solution.py:41
  2.8 0.1 collective-permute-start.1
  2.9 2.7 %pack_last.1 = (bf16[32,2,4352]{2,1,0:T(2,128)(2,1)}, f32[2,4096]{1,0:T(2,128)}) custom-call(s32[1]{0:T(128)} %bitcast.3.dev_ref, s32[64]{0:T(128)} %len_ref.3, bf16[1024,4096]{1,0:T(8,128)(2,1)} %bitcast.36, bf16[1024,4096]{1,0:T(8,128)(2,1)} %bitcast.37, bf16[1,128]{1,0:T(2,128)(2,1)} %ga_ref.1, bf16[1,128]{1,0:T(2,128)(2,1)} %gm_ref.1, bf16[1,128]{1,0:T(2,128)(2,1)} %gf_ref.1), custom_call_target="tpu_custom_call" | custom-call | tf_op jit(solution)/shard_map/pack_last/pallas_call | solution.py:120
  5.7 9.1 %all-to-all-start = ((bf16[32,2,4352]{2,1,0:T(2,128)(2,1)}), bf16[32,2,4352]{2,1,0:T(2,128)(2,1)S(1)}, u32[]{:S(2)}, u32[]{:S(2)}) async-start(bf16[32,2,4352]{2,1,0:T(2,128)(2,1)} %get-tuple-element.15), calls=%async_computation | async-start | bytes 1114112 | tf_op jit(solution)/shard_map/all_to_all | solution.py:65
  14.8 0.2 copy.21
  15.0 0.2 copy.22
  15.2 0.1 fusion.value_ref
  15.3 0.1 multiply_convert_fusion.2
  15.4 0.1 multiply_convert_fusion.1
  15.6 2.8 %collective-permute-start.6 = (bf16[256,512]{1,0:T(8,128)(2,1)S(1)}, bf16[256,512]{1,0:T(8,128)(2,1)S(1)}, u32[]{:S(2)}, u32[]{:S(2)}) collective-permute-start(bf16[256,512]{1,0:T(8,128)(2,1)S(1)} %get-tuple-element.22), channel_id=1, source_target_pairs={{0,2},{1,3},{2,0},{3,1},{4,6},{5,7},{6,4},{7,5},{8,10},{9,11},{10,... | collective-permute-start | bytes 786440 | tf_op jit(solution)/shard_map/ppermute | solution.py:41
  18.4 0.3 collective-permute-start.7
  18.7 2.4 %collective-permute-start.5 = (bf16[256,512]{1,0:T(8,128)(2,1)S(1)}, bf16[256,512]{1,0:T(8,128)(2,1)S(1)}, u32[]{:S(2)}, u32[]{:S(2)}) collective-permute-start(bf16[256,512]{1,0:T(8,128)(2,1)S(1)} %get-tuple-element.22), channel_id=1, source_target_pairs={{0,3},{1,0},{2,1},{3,2},{4,7},{5,4},{6,5},{7,6},{8,11},{9,8},{10,9... | collective-permute-start | bytes 786440 | tf_op jit(solution)/shard_map/ppermute | solution.py:41
  21.1 1.3 collective-permute-start.4
  22.4 2.4 %collective-permute-start.3 = (bf16[256,512]{1,0:T(8,128)(2,1)S(1)}, bf16[256,512]{1,0:T(8,128)(2,1)S(1)}, u32[]{:S(2)}, u32[]{:S(2)}) collective-permute-start(bf16[256,512]{1,0:T(8,128)(2,1)S(1)} %get-tuple-element.23), channel_id=1, source_target_pairs={{0,8},{1,9},{2,10},{3,11},{4,12},{5,13},{6,14},{7,15},{8,0},{9,1},... | collective-permute-start | bytes 786440 | tf_op jit(solution)/shard_map/ppermute | solution.py:41
  24.8 5.5 %collective-permute-done.6 = bf16[256,512]{1,0:T(8,128)(2,1)S(1)} collective-permute-done((bf16[256,512]{1,0:T(8,128)(2,1)S(1)}, bf16[256,512]{1,0:T(8,128)(2,1)S(1)}, u32[]{:S(2)}, u32[]{:S(2)}) %collective-permute-start.6) | collective-permute-done | bytes 262176 | tf_op jit(solution)/shard_map/ppermute | solution.py:41
  30.3 2.8 %collective-permute-start.2 = (bf16[256,512]{1,0:T(8,128)(2,1)S(1)}, bf16[256,512]{1,0:T(8,128)(2,1)}, u32[]{:S(2)}, u32[]{:S(2)}) collective-permute-start(bf16[256,512]{1,0:T(8,128)(2,1)S(1)} %get-tuple-element.23), channel_id=1, source_target_pairs={{0,12},{1,13},{2,14},{3,15},{4,0},{5,1},{6,2},{7,3},{8,4},{9,5},{1... | collective-permute-start | bytes 786440 | tf_op jit(solution)/shard_map/ppermute | solution.py:41
  33.0 3.7 %collective-permute-done.7 = bf16[256,512]{1,0:T(8,128)(2,1)S(1)} collective-permute-done((bf16[256,512]{1,0:T(8,128)(2,1)S(1)}, bf16[256,512]{1,0:T(8,128)(2,1)S(1)}, u32[]{:S(2)}, u32[]{:S(2)}) %collective-permute-start.7) | collective-permute-done | bytes 262176 | tf_op jit(solution)/shard_map/ppermute | solution.py:41
  36.7 1.9 collective-permute-start.10
  38.8 0.2 fusion.11
  39.0 0.1 pad_maximum_fusion.7
  39.2 0.5 collective-permute-start.8
  39.6 1.2 copy-done.10
  40.9 0.8 parcel.1
  41.7 1.0 copy-done.7
  42.7 0.6 copy-done.21
  43.3 0.6 copy-done.23
  43.9 5.6 %all-to-all-start.1 = ((bf16[32,144,128]{2,1,0:T(8,128)(2,1)}), bf16[32,144,128]{2,1,0:T(8,128)(2,1)S(1)}, u32[]{:S(2)}, u32[]{:S(2)}) async-start(bf16[32,144,128]{2,1,0:T(8,128)(2,1)} %copy-done.7), calls=%async_computation.1 | async-start | bytes 2359296 | tf_op jit(solution)/shard_map/all_to_all | solution.py:65
  49.6 1.0 pad_maximum_fusion.a_low
  50.6 1.3 collective-permute-start.9
  51.9 1.2 collective-permute-start.15
  53.1 1.5 collective-permute-start.14
  54.6 1.2 collective-permute-start.13
  55.7 1.5 collective-permute-start.12
  57.2 19.6 %collective-permute-done.9.refs_1_ = bf16[2,256,512]{2,1,0:T(8,128)(2,1)} collective-permute-done((bf16[2,256,512]{2,1,0:T(8,128)(2,1)S(1)}, bf16[2,256,512]{2,1,0:T(8,128)(2,1)}, u32[]{:S(2)}, u32[]{:S(2)}) %collective-permute-start.9) | collective-permute-done | bytes 524320 | tf_op jit(solution)/shard_map/ppermute | solution.py:41
  76.8 2.7 %collective-permute-start.17 = (bf16[2,256,512]{2,1,0:T(8,128)(2,1)}, bf16[2,256,512]{2,1,0:T(8,128)(2,1)}, u32[]{:S(2)}, u32[]{:S(2)}) collective-permute-start(bf16[2,256,512]{2,1,0:T(8,128)(2,1)} %collective-permute-done.10.refs_2_), channel_id=1, source_target_pairs={{0,12},{1,13},{2,14},{3,15},{4,0},{5,1},{6,2},{7,3},{8,4},{9,5},{1... | collective-permute-start | bytes 1572872 | tf_op jit(solution)/shard_map/ppermute | solution.py:41
  79.5 0.8 copy-done.11
  80.3 0.8 copy-done.13
  81.1 0.2 collective-permute-start.19
  81.4 6.7 %collective-permute-done.13.refs_1_ = bf16[2,256,512]{2,1,0:T(8,128)(2,1)S(1)} collective-permute-done((bf16[2,256,512]{2,1,0:T(8,128)(2,1)S(1)}, bf16[2,256,512]{2,1,0:T(8,128)(2,1)S(1)}, u32[]{:S(2)}, u32[]{:S(2)}) %collective-permute-start.13) | collective-permute-done | bytes 524320 | tf_op jit(solution)/shard_map/ppermute | solution.py:41
  88.1 0.8 copy-done.15
  89.0 1.0 fusion.4
  90.0 0.9 pad_maximum_fusion.5
  90.9 6.2 %own_keys.1 = (f32[1024,1024]{1,0:T(8,128)S(1)}, f32[1024,128]{1,0:T(8,128)S(1)}, bf16[1024,4096]{1,0:T(8,128)(2,1)S(1)}) custom-call(s32[4]{0:T(128)S(1)} %pad_add_fusion.dev_ref, bf16[1024,4096]{1,0:T(8,128)(2,1)} %bitcast.38, bf16[2,256,512]{2,1,0:T(8,128)(2,1)S(1)} %pad_maximum_fusion.a_low, bf16[2,256,512]{2,1,0:T(8,128)(2,1)S(1)} %pad_maximum_fusion.1.a_high, ...), custom_call_target="tpu_custom_call" | custom-call | tf_op jit(solution)/shard_map/own_keys/pallas_call | solution.py:241
  97.1 0.8 copy-done.17
  97.9 6.2 %shard_map.149.acc_ref = f32[1024,1024]{1,0:T(8,128)S(1)} custom-call(s32[4]{0:T(128)S(1)} %pad_add_fusion.dev_ref, bf16[1024,4096]{1,0:T(8,128)(2,1)S(1)} %get-tuple-element.12.x_ref, f32[1024,1024]{1,0:T(8,128)S(1)} %get-tuple-element.13.acc_ref, bf16[2,256,512]{2,1,0:T(8,128)(2,1)} %collective-permute-done.8.refs_0_, ...), custom_call_target="tpu_custom_call", output_to_operand_aliasing={{}: (2, {})} | custom-call | tf_op jit(solution)/shard_map/pallas_call | solution.py:257
  104.1 4.1 %shard_map.150.acc_ref = f32[1024,1024]{1,0:T(8,128)S(1)} custom-call(s32[4]{0:T(128)S(1)} %pad_add_fusion.dev_ref, bf16[1024,4096]{1,0:T(8,128)(2,1)S(1)} %get-tuple-element.12.x_ref, f32[1024,1024]{1,0:T(8,128)S(1)} %shard_map.149.acc_ref, bf16[2,256,512]{2,1,0:T(8,128)(2,1)} %collective-permute-done.12.refs_0_, ...), custom_call_target="tpu_custom_call", output_to_operand_aliasing={{}: (2, {})} | custom-call | tf_op jit(solution)/shard_map/pallas_call | solution.py:257
  108.2 3.3 %shard_map.151.acc_ref = f32[1024,1024]{1,0:T(8,128)S(1)} custom-call(s32[4]{0:T(128)S(1)} %pad_add_fusion.dev_ref, bf16[1024,4096]{1,0:T(8,128)(2,1)S(1)} %get-tuple-element.12.x_ref, f32[1024,1024]{1,0:T(8,128)S(1)} %shard_map.150.acc_ref, bf16[2,256,512]{2,1,0:T(8,128)(2,1)} %collective-permute-done.16.refs_0_, ...), custom_call_target="tpu_custom_call", output_to_operand_aliasing={{}: (2, {})} | custom-call | tf_op jit(solution)/shard_map/pallas_call | solution.py:257
  111.5 2.1 copy-done.2
  113.6 3.4 %copy-done.1 = bf16[1024,4096]{1,0:T(8,128)(2,1)S(1)} copy-done((bf16[1024,4096]{1,0:T(8,128)(2,1)S(1)}, bf16[1024,4096]{1,0:T(8,128)(2,1)}, u32[]{:S(2)}) %copy-start.1) | copy-done | bytes 8388632
  117.0 2.2 %copy-done.3 = f32[1024,1024]{1,0:T(8,128)S(1)} copy-done((f32[1024,1024]{1,0:T(8,128)S(1)}, f32[1024,1024]{1,0:T(8,128)}, u32[]{:S(2)}) %copy-start.3) | copy-done | bytes 4194328
  119.2 5.9 %attend.1 = bf16[32,2,4096]{2,1,0:T(2,128)(2,1)S(1)} custom-call(s32[4]{0:T(128)S(1)} %pad_add_fusion.dev_ref, s32[64]{0:T(128)S(1)} %copy-done.25, bf16[1024,4096]{1,0:T(8,128)(2,1)S(1)} %copy-done.1, f32[1024,1024]{1,0:T(8,128)S(1)} %copy-done.3, f32[1024,128]{1,0:T(8,128)S(1)} %copy-done.18, bf16[2,256,512]{2,1,0:T(8,128)(2,1)} %collective-permute-done.18.a_low, ...), custom_call_target="tpu_custom_call" | custom-call | tf_op jit(solution)/shard_map/attend/pallas_call | solution.py:320
  125.2 17.3 %all_to_all.35.x_ref = bf16[32,2,4096]{2,1,0:T(2,128)(2,1)S(1)} all-to-all(bf16[32,2,4096]{2,1,0:T(2,128)(2,1)S(1)} %attend.1), channel_id=1, replica_groups=mesh['judge'=4,'fsdp'=32] {'fsdp'}, dimensions={0} | all-to-all | bytes 1048576 | tf_op jit(solution)/shard_map/all_to_all | solution.py:65
  142.5 0.7 mix.1
  143.2 13.9 %all_to_all.36.parts_ref = bf16[32,2,4096]{2,1,0:T(2,128)(2,1)S(1)} all-to-all(bf16[32,2,4096]{2,1,0:T(2,128)(2,1)S(1)} %mix.1), channel_id=1, replica_groups=mesh['judge'=4,'fsdp'=32] {'fsdp'}, dimensions={0} | all-to-all | bytes 1048576 | tf_op jit(solution)/shard_map/all_to_all | solution.py:65
  157.1 0.3 middle.1
  157.4 12.6 %all_to_all.37.x_ref = bf16[32,2,4096]{2,1,0:T(2,128)(2,1)S(1)} all-to-all(bf16[32,2,4096]{2,1,0:T(2,128)(2,1)S(1)} %get-tuple-element.19), channel_id=1, replica_groups=mesh['judge'=4,'fsdp'=32] {'fsdp'}, dimensions={0} | all-to-all | bytes 1048576 | tf_op jit(solution)/shard_map/all_to_all | solution.py:65
  170.1 2.9 %mlp.1 = bf16[32,2,4096]{2,1,0:T(2,128)(2,1)S(1)} custom-call(bf16[32,2,4096]{2,1,0:T(2,128)(2,1)S(1)} %all_to_all.37.x_ref, bf16[448,4096]{1,0:T(8,128)(2,1)S(1)} %bitcast.31, bf16[448,4096]{1,0:T(8,128)(2,1)S(1)} %bitcast.32, bf16[448,4096]{1,0:T(8,128)(2,1)S(1)} %bitcast.33), custom_call_target="tpu_custom_call" | custom-call | tf_op jit(solution)/shard_map/mlp/pallas_call | solution.py:394
  172.9 13.0 %all_to_all.38.parts_ref = bf16[32,2,4096]{2,1,0:T(2,128)(2,1)S(1)} all-to-all(bf16[32,2,4096]{2,1,0:T(2,128)(2,1)S(1)} %mlp.1), channel_id=1, replica_groups=mesh['judge'=4,'fsdp'=32] {'fsdp'}, dimensions={0} | all-to-all | bytes 1048576 | tf_op jit(solution)/shard_map/all_to_all | solution.py:65
  186.0 0.3 finish.1
  186.3 21.7 %all_to_all.39 = f32[128,1,384]{2,1,0:T(1,128)S(1)} all-to-all(f32[128,1,384]{2,1,0:T(1,128)S(1)} %finish.1), channel_id=1, replica_groups=mesh['judge'=4,'fsdp'=32] {'judge','fsdp'}, dimensions={0} | all-to-all | bytes 393216 | tf_op jit(solution)/shard_map/all_to_all | solution.py:65
  208.1 0.1 reshape.57
  208.2 0.2 fusion.5
  208.4 0.2 fusion.6
  208.6 0.9 fusion.7
  (89 shorter events, 0.6 us)
Async XLA Ops:
  0.6 14.8 %collective-permute-start = (bf16[128,1024]{1,0:T(8,128)(2,1)}, bf16[128,1024]{1,0:T(8,128)(2,1)S(1)}, u32[]{:S(2)}, u32[]{:S(2)}) collective-permute-start(bf16[128,1024]{1,0:T(8,128)(2,1)} %bitcast.43), channel_id=1, source_target_pairs={{0,16},{1,17},{2,18},{3,19},{4,20},{5,21},{6,22},{7,23},{8,24},{9,... | collective-permute-start | bytes 786440 | tf_op jit(solution)/shard_map/ppermute | solution.py:41
  2.8 12.6 %collective-permute-start.1 = (bf16[128]{0:T(256)(128)(2,1)}, bf16[128]{0:T(256)(128)(2,1)S(1)}, u32[]{:S(2)}, u32[]{:S(2)}) collective-permute-start(bf16[128]{0:T(256)(128)(2,1)} %bitcast.49), channel_id=1, source_target_pairs={{0,16},{1,17},{2,18},{3,19},{4,20},{5,21},{6,22},{7,23},{8,24},{9,... | collective-permute-start | bytes 776 | tf_op jit(solution)/shard_map/ppermute | solution.py:41
  2.9 11.9 %copy-start.29 = (bf16[1,128]{1,0:T(2,128)(2,1)S(1)}, bf16[1,128]{1,0:T(2,128)(2,1)}, u32[]{:S(2)}) copy-start(bf16[1,128]{1,0:T(2,128)(2,1)} %ga_ref.1) | copy-start | bytes 772
  2.9 11.9 %copy-start.27 = (bf16[1,128,1024]{2,1,0:T(8,128)(2,1)S(1)}, bf16[1,128,1024]{2,1,0:T(8,128)(2,1)}, u32[]{:S(2)}) copy-start(bf16[1,128,1024]{2,1,0:T(8,128)(2,1)} %param.20) | copy-start | bytes 786436
  2.9 12.4 %copy-start.26 = (bf16[1,128,1024]{2,1,0:T(8,128)(2,1)S(1)}, bf16[1,128,1024]{2,1,0:T(8,128)(2,1)}, u32[]{:S(2)}) copy-start(bf16[1,128,1024]{2,1,0:T(8,128)(2,1)} %param.19) | copy-start | bytes 786436
  5.7 15.4 %copy-start.25 = (s32[64]{0:T(128)S(1)}, s32[64]{0:T(128)}, u32[]{:S(2)}) copy-start(s32[64]{0:T(128)} %len_ref.3) | copy-start | bytes 772
  5.7 34.0 %all-to-all-start = ((bf16[32,2,4352]{2,1,0:T(2,128)(2,1)}), bf16[32,2,4352]{2,1,0:T(2,128)(2,1)S(1)}, u32[]{:S(2)}, u32[]{:S(2)}) async-start(bf16[32,2,4352]{2,1,0:T(2,128)(2,1)} %get-tuple-element.15), calls=%async_computation | async-start | bytes 1114112 | tf_op jit(solution)/shard_map/all_to_all | solution.py:65
  15.6 14.7 %collective-permute-start.6 = (bf16[256,512]{1,0:T(8,128)(2,1)S(1)}, bf16[256,512]{1,0:T(8,128)(2,1)S(1)}, u32[]{:S(2)}, u32[]{:S(2)}) collective-permute-start(bf16[256,512]{1,0:T(8,128)(2,1)S(1)} %get-tuple-element.22), channel_id=1, source_target_pairs={{0,2},{1,3},{2,0},{3,1},{4,6},{5,7},{6,4},{7,5},{8,10},{9,11},{10,... | collective-permute-start | bytes 786440 | tf_op jit(solution)/shard_map/ppermute | solution.py:41
  18.4 18.3 %collective-permute-start.7 = (bf16[256,512]{1,0:T(8,128)(2,1)S(1)}, bf16[256,512]{1,0:T(8,128)(2,1)S(1)}, u32[]{:S(2)}, u32[]{:S(2)}) collective-permute-start(bf16[256,512]{1,0:T(8,128)(2,1)S(1)} %get-tuple-element.22), channel_id=1, source_target_pairs={{0,1},{1,2},{2,3},{3,0},{4,5},{5,6},{6,7},{7,4},{8,9},{9,10},{10,1... | collective-permute-start | bytes 786440 | tf_op jit(solution)/shard_map/ppermute | solution.py:41
  18.7 20.0 %collective-permute-start.5 = (bf16[256,512]{1,0:T(8,128)(2,1)S(1)}, bf16[256,512]{1,0:T(8,128)(2,1)S(1)}, u32[]{:S(2)}, u32[]{:S(2)}) collective-permute-start(bf16[256,512]{1,0:T(8,128)(2,1)S(1)} %get-tuple-element.22), channel_id=1, source_target_pairs={{0,3},{1,0},{2,1},{3,2},{4,7},{5,4},{6,5},{7,6},{8,11},{9,8},{10,9... | collective-permute-start | bytes 786440 | tf_op jit(solution)/shard_map/ppermute | solution.py:41
  21.1 18.0 %collective-permute-start.4 = (bf16[256,512]{1,0:T(8,128)(2,1)S(1)}, bf16[256,512]{1,0:T(8,128)(2,1)S(1)}, u32[]{:S(2)}, u32[]{:S(2)}) collective-permute-start(bf16[256,512]{1,0:T(8,128)(2,1)S(1)} %get-tuple-element.23), channel_id=1, source_target_pairs={{0,4},{1,5},{2,6},{3,7},{4,8},{5,9},{6,10},{7,11},{8,12},{9,13},{1... | collective-permute-start | bytes 786440 | tf_op jit(solution)/shard_map/ppermute | solution.py:41
  22.4 16.8 %collective-permute-start.3 = (bf16[256,512]{1,0:T(8,128)(2,1)S(1)}, bf16[256,512]{1,0:T(8,128)(2,1)S(1)}, u32[]{:S(2)}, u32[]{:S(2)}) collective-permute-start(bf16[256,512]{1,0:T(8,128)(2,1)S(1)} %get-tuple-element.23), channel_id=1, source_target_pairs={{0,8},{1,9},{2,10},{3,11},{4,12},{5,13},{6,14},{7,15},{8,0},{9,1},... | collective-permute-start | bytes 786440 | tf_op jit(solution)/shard_map/ppermute | solution.py:41
  30.3 19.3 %collective-permute-start.2 = (bf16[256,512]{1,0:T(8,128)(2,1)S(1)}, bf16[256,512]{1,0:T(8,128)(2,1)}, u32[]{:S(2)}, u32[]{:S(2)}) collective-permute-start(bf16[256,512]{1,0:T(8,128)(2,1)S(1)} %get-tuple-element.23), channel_id=1, source_target_pairs={{0,12},{1,13},{2,14},{3,15},{4,0},{5,1},{6,2},{7,3},{8,4},{9,5},{1... | collective-permute-start | bytes 786440 | tf_op jit(solution)/shard_map/ppermute | solution.py:41
  36.7 16.3 %collective-permute-start.10 = (bf16[2,256,512]{2,1,0:T(8,128)(2,1)S(1)}, bf16[2,256,512]{2,1,0:T(8,128)(2,1)}, u32[]{:S(2)}, u32[]{:S(2)}) collective-permute-start(bf16[2,256,512]{2,1,0:T(8,128)(2,1)S(1)} %pad_maximum_fusion.3.b_high), channel_id=1, source_target_pairs={{0,12},{1,13},{2,14},{3,15},{4,0},{5,1},{6,2},{7,3},{8,4},{9,5},{1... | collective-permute-start | bytes 1572872 | tf_op jit(solution)/shard_map/ppermute | solution.py:41
  38.7 15.8 %collective-permute-start.11 = (bf16[2,256,512]{2,1,0:T(8,128)(2,1)S(1)}, bf16[2,256,512]{2,1,0:T(8,128)(2,1)}, u32[]{:S(2)}, u32[]{:S(2)}) collective-permute-start(bf16[2,256,512]{2,1,0:T(8,128)(2,1)S(1)} %pad_maximum_fusion.2.b_low), channel_id=1, source_target_pairs={{0,4},{1,5},{2,6},{3,7},{4,8},{5,9},{6,10},{7,11},{8,12},{9,13},{1... | collective-permute-start | bytes 1572872 | tf_op jit(solution)/shard_map/ppermute | solution.py:41
  39.2 16.6 %collective-permute-start.8 = (bf16[2,256,512]{2,1,0:T(8,128)(2,1)S(1)}, bf16[2,256,512]{2,1,0:T(8,128)(2,1)}, u32[]{:S(2)}, u32[]{:S(2)}) collective-permute-start(bf16[2,256,512]{2,1,0:T(8,128)(2,1)S(1)} %pad_maximum_fusion.1.a_high), channel_id=1, source_target_pairs={{0,3},{1,0},{2,1},{3,2},{4,7},{5,4},{6,5},{7,6},{8,11},{9,8},{10,9... | collective-permute-start | bytes 1572872 | tf_op jit(solution)/shard_map/ppermute | solution.py:41
  39.6 1.2 copy-start.10
  41.7 1.0 copy-start.7
  42.7 0.6 copy-start.21
  43.3 0.6 copy-start.23
  43.9 69.7 %all-to-all-start.1 = ((bf16[32,144,128]{2,1,0:T(8,128)(2,1)}), bf16[32,144,128]{2,1,0:T(8,128)(2,1)S(1)}, u32[]{:S(2)}, u32[]{:S(2)}) async-start(bf16[32,144,128]{2,1,0:T(8,128)(2,1)} %copy-done.7), calls=%async_computation.1 | async-start | bytes 2359296 | tf_op jit(solution)/shard_map/all_to_all | solution.py:65
  50.6 26.2 %collective-permute-start.9 = (bf16[2,256,512]{2,1,0:T(8,128)(2,1)S(1)}, bf16[2,256,512]{2,1,0:T(8,128)(2,1)}, u32[]{:S(2)}, u32[]{:S(2)}) collective-permute-start(bf16[2,256,512]{2,1,0:T(8,128)(2,1)S(1)} %pad_maximum_fusion.a_low), channel_id=1, source_target_pairs={{0,1},{1,2},{2,3},{3,0},{4,5},{5,6},{6,7},{7,4},{8,9},{9,10},{10,1... | collective-permute-start | bytes 1572872 | tf_op jit(solution)/shard_map/ppermute | solution.py:41
  51.9 27.7 %collective-permute-start.15 = (bf16[2,256,512]{2,1,0:T(8,128)(2,1)S(1)}, bf16[2,256,512]{2,1,0:T(8,128)(2,1)S(1)}, u32[]{:S(2)}, u32[]{:S(2)}) collective-permute-start(bf16[2,256,512]{2,1,0:T(8,128)(2,1)S(1)} %pad_maximum_fusion.3.b_high), channel_id=1, source_target_pairs={{0,4},{1,5},{2,6},{3,7},{4,8},{5,9},{6,10},{7,11},{8,12},{9,13},{1... | collective-permute-start | bytes 1572872 | tf_op jit(solution)/shard_map/ppermute | solution.py:41
  53.1 27.3 %collective-permute-start.14 = (bf16[2,256,512]{2,1,0:T(8,128)(2,1)S(1)}, bf16[2,256,512]{2,1,0:T(8,128)(2,1)S(1)}, u32[]{:S(2)}, u32[]{:S(2)}) collective-permute-start(bf16[2,256,512]{2,1,0:T(8,128)(2,1)S(1)} %pad_maximum_fusion.2.b_low), channel_id=1, source_target_pairs={{0,12},{1,13},{2,14},{3,15},{4,0},{5,1},{6,2},{7,3},{8,4},{9,5},{1... | collective-permute-start | bytes 1572872 | tf_op jit(solution)/shard_map/ppermute | solution.py:41
  54.6 33.5 %collective-permute-start.13 = (bf16[2,256,512]{2,1,0:T(8,128)(2,1)S(1)}, bf16[2,256,512]{2,1,0:T(8,128)(2,1)S(1)}, u32[]{:S(2)}, u32[]{:S(2)}) collective-permute-start(bf16[2,256,512]{2,1,0:T(8,128)(2,1)S(1)} %pad_maximum_fusion.1.a_high), channel_id=1, source_target_pairs={{0,1},{1,2},{2,3},{3,0},{4,5},{5,6},{6,7},{7,4},{8,9},{9,10},{10,1... | collective-permute-start | bytes 1572872 | tf_op jit(solution)/shard_map/ppermute | solution.py:41
  55.7 48.3 %collective-permute-start.12 = (bf16[2,256,512]{2,1,0:T(8,128)(2,1)S(1)}, bf16[2,256,512]{2,1,0:T(8,128)(2,1)}, u32[]{:S(2)}, u32[]{:S(2)}) collective-permute-start(bf16[2,256,512]{2,1,0:T(8,128)(2,1)S(1)} %pad_maximum_fusion.a_low), channel_id=1, source_target_pairs={{0,3},{1,0},{2,1},{3,2},{4,7},{5,4},{6,5},{7,6},{8,11},{9,8},{10,9... | collective-permute-start | bytes 1572872 | tf_op jit(solution)/shard_map/ppermute | solution.py:41
  76.8 31.4 %collective-permute-start.17 = (bf16[2,256,512]{2,1,0:T(8,128)(2,1)}, bf16[2,256,512]{2,1,0:T(8,128)(2,1)}, u32[]{:S(2)}, u32[]{:S(2)}) collective-permute-start(bf16[2,256,512]{2,1,0:T(8,128)(2,1)} %collective-permute-done.10.refs_2_), channel_id=1, source_target_pairs={{0,12},{1,13},{2,14},{3,15},{4,0},{5,1},{6,2},{7,3},{8,4},{9,5},{1... | collective-permute-start | bytes 1572872 | tf_op jit(solution)/shard_map/ppermute | solution.py:41
  79.5 0.8 copy-start.11
  80.3 27.9 %collective-permute-start.16 = (bf16[2,256,512]{2,1,0:T(8,128)(2,1)}, bf16[2,256,512]{2,1,0:T(8,128)(2,1)}, u32[]{:S(2)}, u32[]{:S(2)}) collective-permute-start(bf16[2,256,512]{2,1,0:T(8,128)(2,1)} %collective-permute-done.11.refs_3_), channel_id=1, source_target_pairs={{0,4},{1,5},{2,6},{3,7},{4,8},{5,9},{6,10},{7,11},{8,12},{9,13},{1... | collective-permute-start | bytes 1572872 | tf_op jit(solution)/shard_map/ppermute | solution.py:41
  80.3 0.8 copy-start.13
  81.1 32.5 %collective-permute-start.19 = (bf16[2,256,512]{2,1,0:T(8,128)(2,1)}, bf16[2,256,512]{2,1,0:T(8,128)(2,1)}, u32[]{:S(2)}, u32[]{:S(2)}) collective-permute-start(bf16[2,256,512]{2,1,0:T(8,128)(2,1)} %collective-permute-done.8.refs_0_), channel_id=1, source_target_pairs={{0,3},{1,0},{2,1},{3,2},{4,7},{5,4},{6,5},{7,6},{8,11},{9,8},{10,9... | collective-permute-start | bytes 1572872 | tf_op jit(solution)/shard_map/ppermute | solution.py:41
  88.1 0.9 copy-start.15
  88.9 24.7 %collective-permute-start.18 = (bf16[2,256,512]{2,1,0:T(8,128)(2,1)}, bf16[2,256,512]{2,1,0:T(8,128)(2,1)}, u32[]{:S(2)}, u32[]{:S(2)}) collective-permute-start(bf16[2,256,512]{2,1,0:T(8,128)(2,1)} %collective-permute-done.9.refs_1_), channel_id=1, source_target_pairs={{0,1},{1,2},{2,3},{3,0},{4,5},{5,6},{6,7},{7,4},{8,9},{9,10},{10,1... | collective-permute-start | bytes 1572872 | tf_op jit(solution)/shard_map/ppermute | solution.py:41
  97.1 0.8 copy-start.17
  97.9 10.4 %copy-start = (bf16[1024,4096]{1,0:T(8,128)(2,1)}, bf16[1024,4096]{1,0:T(8,128)(2,1)S(1)}, u32[]{:S(2)}) copy-start(bf16[1024,4096]{1,0:T(8,128)(2,1)S(1)} %get-tuple-element.12.x_ref) | copy-start | bytes 25165828
  97.9 6.2 %copy-start.12 = (bf16[2,256,512]{2,1,0:T(8,128)(2,1)S(1)}, bf16[2,256,512]{2,1,0:T(8,128)(2,1)}, u32[]{:S(2)}) copy-start(bf16[2,256,512]{2,1,0:T(8,128)(2,1)} %copy-done.11) | copy-start | bytes 1572868
  97.9 6.2 %copy-start.14 = (bf16[2,256,512]{2,1,0:T(8,128)(2,1)S(1)}, bf16[2,256,512]{2,1,0:T(8,128)(2,1)}, u32[]{:S(2)}) copy-start(bf16[2,256,512]{2,1,0:T(8,128)(2,1)} %copy-done.13) | copy-start | bytes 1572868
  97.9 6.2 %copy-start.16 = (bf16[2,256,512]{2,1,0:T(8,128)(2,1)S(1)}, bf16[2,256,512]{2,1,0:T(8,128)(2,1)}, u32[]{:S(2)}) copy-start(bf16[2,256,512]{2,1,0:T(8,128)(2,1)} %copy-done.15) | copy-start | bytes 1572868
  108.2 5.4 %copy-start.8 = (f32[512,128]{1,0:T(8,128)S(1)}, f32[512,128]{1,0:T(8,128)}, u32[]{:S(2)}) copy-start(f32[512,128]{1,0:T(8,128)} %get-tuple-element.33.sin_ref) | copy-start | bytes 786436
  108.2 5.4 %copy-start.18 = (f32[1024,128]{1,0:T(8,128)S(1)}, f32[1024,128]{1,0:T(8,128)}, u32[]{:S(2)}) copy-start(f32[1024,128]{1,0:T(8,128)} %copy-done.17) | copy-start | bytes 1572868
  111.5 2.1 copy-start.2
  113.6 3.4 %copy-start.1 = (bf16[1024,4096]{1,0:T(8,128)(2,1)S(1)}, bf16[1024,4096]{1,0:T(8,128)(2,1)}, u32[]{:S(2)}) copy-start(bf16[1024,4096]{1,0:T(8,128)(2,1)} %copy-done) | copy-start | bytes 25165828
  117.0 2.2 %copy-start.3 = (f32[1024,1024]{1,0:T(8,128)S(1)}, f32[1024,1024]{1,0:T(8,128)}, u32[]{:S(2)}) copy-start(f32[1024,1024]{1,0:T(8,128)} %copy-done.2) | copy-start | bytes 12582916
  119.2 23.3 %copy-start.9 = (bf16[1,128,4096]{2,1,0:T(8,128)(2,1)S(1)}, bf16[1,128,4096]{2,1,0:T(8,128)(2,1)}, u32[]{:S(2)}) copy-start(bf16[1,128,4096]{2,1,0:T(8,128)(2,1)} %param.21) | copy-start | bytes 3145732
  119.2 50.8 %copy-start.5 = (bf16[1,4096,448]{1,2,0:T(8,128)(2,1)S(1)}, bf16[1,4096,448]{1,2,0:T(8,128)(2,1)}, u32[]{:S(2)}) copy-start(bf16[1,4096,448]{1,2,0:T(8,128)(2,1)} %param.24) | copy-start | bytes 11010052
  119.2 50.8 %copy-start.6 = (bf16[1,448,4096]{2,1,0:T(8,128)(2,1)S(1)}, bf16[1,448,4096]{2,1,0:T(8,128)(2,1)}, u32[]{:S(2)}) copy-start(bf16[1,448,4096]{2,1,0:T(8,128)(2,1)} %param.25) | copy-start | bytes 11010052
  125.1 32.0 %copy-start.19 = (f32[2,4096]{1,0:T(2,128)S(1)}, f32[2,4096]{1,0:T(2,128)}, u32[]{:S(2)}) copy-start(f32[2,4096]{1,0:T(2,128)} %get-tuple-element.17.own_ref) | copy-start | bytes 98308
  125.1 32.0 %copy-start.24 = (f32[1,4096]{1,0:T(1,128)S(1)}, f32[1,4096]{1,0:T(1,128)}, u32[]{:S(2)}) copy-start(f32[1,4096]{1,0:T(1,128)} %copy-done.23) | copy-start | bytes 49156
  125.1 44.9 %copy-start.4 = (bf16[1,4096,448]{1,2,0:T(8,128)(2,1)S(1)}, bf16[1,4096,448]{1,2,0:T(8,128)(2,1)}, u32[]{:S(2)}) copy-start(bf16[1,4096,448]{1,2,0:T(8,128)(2,1)} %param.23) | copy-start | bytes 11010052
  170.0 16.0 %copy-start.20 = (f32[1,4096]{1,0:T(1,128)S(1)}, f32[1,4096]{1,0:T(1,128)}, u32[]{:S(2)}) copy-start(f32[1,4096]{1,0:T(1,128)} %head_ref.1) | copy-start | bytes 49156
  170.0 15.9 %copy-start.22 = (f32[1,4096]{1,0:T(1,128)S(1)}, f32[1,4096]{1,0:T(1,128)}, u32[]{:S(2)}) copy-start(f32[1,4096]{1,0:T(1,128)} %copy-done.21) | copy-start | bytes 49156
  170.1 38.1 %copy-start.28 = (s32[64]{0:T(128)S(1)}, s32[64]{0:T(128)}, u32[]{:S(2)}) copy-start(s32[64]{0:T(128)} %param.16) | copy-start | bytes 772
  208.6 0.9 copy-start.30
